TPU v7x, 128 devices: a whole 4x4x4 slice. The times are simulated.
128 devices in a mesh: stn: 8 (over x_hi, y), tm: 16 (over x_lo, z, core).
Axes of the slice: x: 4 (x_hi: 2, x_lo: 2; x = x_hi * 2 + x_lo), y: 4, z: 4, core: 2. Of those that a mesh axis runs over, the one named last changes fastest.
Arguments:
- voltages: bfloat16 [512, 256, 4096], P('stn', 'tm'), may hold values from -52 to 52
- pfb_taps: float32 [16, 4096], replicated, may hold values from -1.5 to 1.5
- eq_gains: float32 [512, 2048], P('stn'), may hold values from 0.5 to 11
Outputs:
- visibilities: float32 [2048, 512, 512], P(('stn', 'tm'))
All inputs are finite; a program needn't handle non-finite values.
Results may differ from a plain program's by a relative error of at most 0.0014.
Values may be sent and summed in bfloat16 or wider, within the bound.
No kernel may reach another device: no remote copies, remote signals or barrier semaphores. Data moves between devices by JAX's collectives and lax.ppermute only.
A program may use at most 448 MiB of HBM per device.

v0:
```python
import math

import jax
import jax.numpy as jnp
from jax import lax
from jax.sharding import PartitionSpec as P


def from_behind(value, axis, steps):
    count = lax.axis_size(axis)
    first, last = (max(0, -steps), min(count, count - steps))
    return lax.ppermute(value, axis, [(source, source + steps) for source in range(first, last)])


def cos_sin(numer, denom):
    angle = 2.0 * math.pi / denom * (numer % denom).astype(jnp.float32)
    return (jnp.cos(angle), jnp.sin(angle))


def transform(filtered, channels):
    inputs_dev, frames_dev, length = filtered.shape
    inner_len = 64
    outer_len = length // inner_len
    kept_upper = channels // outer_len
    row_count = inputs_dev * frames_dev
    highest = lax.Precision.HIGHEST
    arranged = filtered.reshape(row_count, outer_len, inner_len)
    freq_one = lax.broadcasted_iota(jnp.int32, (outer_len, outer_len), 0)
    time_one = lax.broadcasted_iota(jnp.int32, (outer_len, outer_len), 1)
    cos_one, sin_one = cos_sin(freq_one * time_one, outer_len)
    section_one = jnp.stack([cos_one, -sin_one])
    partial_ft = jnp.einsum("qka,Rab->qkbR", section_one, arranged, precision=highest)
    freq_twist = lax.broadcasted_iota(jnp.int32, (outer_len, inner_len), 0)
    time_twist = lax.broadcasted_iota(jnp.int32, (outer_len, inner_len), 1)
    twist_cos, twist_sin = cos_sin(freq_twist * time_twist, length)
    twist_table = jnp.stack([jnp.stack([twist_cos, twist_sin]), jnp.stack([-twist_sin, twist_cos])])
    freq_two = lax.broadcasted_iota(jnp.int32, (kept_upper, inner_len), 0)
    time_two = lax.broadcasted_iota(jnp.int32, (kept_upper, inner_len), 1)
    cos_two, sin_two = cos_sin(freq_two * time_two, inner_len)
    section_two = jnp.stack(
        [jnp.stack([cos_two, sin_two], axis=1), jnp.stack([-sin_two, cos_two], axis=1)]
    )
    combined = jnp.einsum("qjrb,rskb->qjksb", section_two, twist_table, precision=highest)
    spectrum = jnp.einsum("qjksb,skbR->qjkR", combined, partial_ft, precision=highest)
    return spectrum.reshape(2, channels, row_count)


def per_device(voltages, pfb_taps, eq_gains):
    tap_count = pfb_taps.shape[0]
    history_len = tap_count - 1
    inputs_dev, frames_dev, length = voltages.shape
    channels = eq_gains.shape[1]
    station_groups = lax.axis_size("stn")
    time_groups = lax.axis_size("tm")
    per_group = channels // (station_groups * time_groups)
    all_inputs = inputs_dev * station_groups
    all_frames = frames_dev * time_groups
    earlier = from_behind(voltages[:, frames_dev - history_len :, :], "tm", 1)
    extended = jnp.concatenate([earlier, voltages], axis=1).astype(jnp.float32)
    kernel = jnp.flip(pfb_taps, axis=0)[:, None, :]
    filtered = lax.conv_general_dilated(
        extended,
        kernel,
        (1,),
        "VALID",
        dimension_numbers=("NWC", "WIO", "NWC"),
        feature_group_count=length,
        precision=lax.Precision.HIGHEST,
    )
    spectrum = transform(filtered, channels)
    gains_turned = jnp.transpose(eq_gains)
    spectra = (
        spectrum.reshape(2, channels, inputs_dev, frames_dev) * gains_turned[None, :, :, None]
    ).astype(jnp.bfloat16)
    shaped = spectra.reshape(2, station_groups * time_groups, per_group, inputs_dev * frames_dev)
    turned = lax.all_to_all(shaped, ("stn", "tm"), split_axis=1, concat_axis=1, tiled=True)
    blocks = turned.reshape(2, station_groups, time_groups, per_group, inputs_dev, frames_dev)
    columns = jnp.transpose(blocks, (0, 3, 1, 4, 2, 5)).reshape(
        2, per_group, all_inputs, all_frames
    )
    swapped = jnp.stack([columns[1], -columns[0]])
    vis_real = jnp.einsum("rcnt,rcmt->cnm", columns, columns, preferred_element_type=jnp.float32)
    vis_imag = jnp.einsum("rcnt,rcmt->cnm", swapped, columns, preferred_element_type=jnp.float32)
    local_power = jnp.sum(jnp.diagonal(vis_real, axis1=1, axis2=2), axis=0)
    power = lax.psum(local_power, ("stn", "tm"))
    scale = lax.rsqrt(power / (all_frames * channels) + 1e-06)
    weight = scale[:, None] * scale[None, :] / all_frames
    row_ids = lax.broadcasted_iota(jnp.int32, (all_inputs, all_inputs), 0)
    col_ids = lax.broadcasted_iota(jnp.int32, (all_inputs, all_inputs), 1)
    lower = row_ids >= col_ids
    return jnp.where(lower[None], vis_real, vis_imag) * weight[None]


def solution(mesh):
    in_specs = (P("stn", "tm", None), P(), P("stn", None))
    out_specs = P(("stn", "tm"), None, None)
    return jax.shard_map(
        per_device, mesh=mesh, in_specs=in_specs, out_specs=out_specs, check_vma=False
    )
```

profile of v0, /device:TPU:1, one launch (start us, length us, event | category | flops | bytes accessed | tf_op | source)
XLA Modules:
  0.0 891.8 jit_solution(8095447733145545676)
XLA Ops:
  0.0 11.4 %copy.46 = bf16[64,16,4096]{2,0,1:T(8,128)(2,1)} copy(bf16[64,16,4096]{2,1,0:T(8,128)(2,1)} %param.3) | data formatting | bytes 16777216 | tf_op args[0]
  11.4 7.4 slice.19
  24.7 5.3 convolution_bitcast_fusion.2
  29.9 6.8 copy.54
  37.6 21.5 %mul.180 = f32[2048,64,16]{2,1,0:T(8,128)} broadcast(f32[2048,64]{1,0:T(8,128)S(1)} %copy.56), dimensions={0,1} | broadcast | bytes 8912896 | tf_op jit(solution)/shard_map/mul | solution.py:73
  59.0 54.5 %mul.181 = f32[128,16,1024]{2,1,0:T(8,128)} reshape(f32[2048,64,16]{2,1,0:T(8,128)} %mul.180) | data formatting | bytes 16777216 | tf_op jit(solution)/shard_map/mul | solution.py:73
  114.3 22.0 %fusion.3 = f32[64,16,4096]{2,0,1:T(8,128)S(1)} fusion(bf16[64,16,4096]{2,0,1:T(8,128)(2,1)} %copy.46, bf16[64,15,4096]{2,0,1:T(8,128)(2,1)} %collective-permute-done, f32[16,1,4096]{2,0,1:T(8,128)S(1)} %bitcast.69), kind=kOutput, calls=%fused_computation.6 | convolution fusion | flops 813432832 | bytes 33292288 | tf_op jit(solution)/shard_map/conv_general_dilated | solution.py:61
  136.4 18.8 %copy.49 = f32[64,16,4096]{2,1,0:T(8,128)} copy(f32[64,16,4096]{2,0,1:T(8,128)S(1)} %fusion.3) | data formatting | bytes 33554432 | tf_op jit(solution)/shard_map/conv_general_dilated | solution.py:61
  155.2 27.0 %reshape.234 = f32[1024,64,64]{2,1,0:T(8,128)} reshape(f32[64,16,4096]{2,1,0:T(8,128)} %copy.49) | data formatting | bytes 33554432 | tf_op jit(solution)/shard_map/reshape | solution.py:27
  182.2 26.2 %copy.69 = f32[1024,64,64,1]{0,1,3,2:T(8,128)} copy(f32[1024,64,64,1]{2,1,0,3:T(8,128)} %bitcast.62) | data formatting | bytes 33554432 | tf_op jit(solution)/shard_map/reshape | solution.py:27
  208.4 33.7 %convolution_bitcast_fusion = f32[2,64,64,1024,1]{3,1,0,2,4:T(8,128)} fusion(f32[1024,64,64,1]{0,1,3,2:T(8,128)} %copy.69, f32[1,64,64]{2,1,0:T(8,128)S(1)} %copy-done.5, f32[1,64,64]{2,1,0:T(8,128)S(1)} %copy-done.6), kind=kOutput, calls=%fused_computation.10 | convolution fusion | flops 6442459136 | bytes 50364416 | tf_op jit(solution)/shard_map/qka,Rab->qkbR/dot_general | solution.py:32
  242.1 47.6 %fusion.7 = f32[2,32,64,1024]{3,1,0,2:T(8,128)} fusion(f32[2,32,64,2,64]{4,1,3,0,2:T(8,128)S(1)} %copy-done.1, f32[2,64,64,1024,1]{3,1,0,2,4:T(8,128)} %convolution_bitcast_fusion), kind=kOutput, calls=%fused_computation.11 | convolution fusion | flops 6442450944 | bytes 52428800 | tf_op jit(solution)/shard_map/qjksb,skbR->qjkR/dot_general | solution.py:44
  289.7 15.6 %copy.55 = f32[2,32,64,1024]{3,2,1,0:T(8,128)S(1)} copy(f32[2,32,64,1024]{3,1,0,2:T(8,128)} %fusion.7) | data formatting | bytes 33554432 | tf_op jit(solution)/shard_map/qjksb,skbR->qjkR/transpose | solution.py:44
  310.5 8.5 copy.57
  319.0 10.1 %all-to-all-start = ((bf16[2,128,16,1024]{3,2,0,1:T(8,128)(2,1)}), bf16[2,128,16,1024]{3,2,0,1:T(8,128)(2,1)}, u32[]{:S(2)}, u32[]{:S(2)}) async-start(bf16[2,128,16,1024]{3,2,0,1:T(8,128)(2,1)} %copy.57), calls=%async_computation | async-start | bytes 16777216 | tf_op jit(solution)/shard_map/all_to_all | solution.py:76
  330.4 100.1 %all-to-all-done = bf16[2,128,16,1024]{3,2,0,1:T(8,128)(2,1)} async-done(((bf16[2,128,16,1024]{3,2,0,1:T(8,128)(2,1)}), bf16[2,128,16,1024]{3,2,0,1:T(8,128)(2,1)}, u32[]{:S(2)}, u32[]{:S(2)}) %all-to-all-start) | async-done | bytes 8388640 | tf_op jit(solution)/shard_map/all_to_all | solution.py:76
  430.5 62.1 %reshape.251 = bf16[2,8,16,16,64,16]{5,4,3,0,2,1:T(8,128)(2,1)} reshape(bf16[2,128,16,1024]{3,2,0,1:T(8,128)(2,1)} %all-to-all-done) | data formatting | bytes 16777216 | tf_op jit(solution)/shard_map/reshape | solution.py:77
  492.6 56.9 %copy.59 = bf16[2,8,16,16,64,16]{4,5,2,1,3,0:T(8,128)(2,1)} copy(bf16[2,8,16,16,64,16]{5,4,3,0,2,1:T(8,128)(2,1)} %reshape.251) | data formatting | bytes 16777216 | tf_op jit(solution)/shard_map/reshape | solution.py:77
  549.5 57.9 %copy.60 = bf16[2,16,8,64,16,16]{3,2,5,4,1,0:T(8,128)(2,1)} copy(bf16[2,16,8,64,16,16]{5,3,1,0,4,2:T(8,128)(2,1)} %bitcast.18) | data formatting | bytes 16777216 | tf_op jit(solution)/shard_map/transpose | solution.py:78
  607.4 22.5 %reshape.236 = bf16[2,16,512,256]{2,3,1,0:T(8,128)(2,1)} reshape(bf16[2,16,8,64,16,16]{3,2,5,4,1,0:T(8,128)(2,1)} %copy.60) | data formatting | bytes 16777216 | tf_op jit(solution)/shard_map/reshape | solution.py:78
  629.9 16.5 %convolution_bitcast_fusion.1 = f32[16,512,512]{2,1,0:T(8,128)} fusion(bf16[2,16,512,256]{2,3,1,0:T(8,128)(2,1)} %reshape.236), kind=kOutput, calls=%fused_computation.12 | convolution fusion | flops 4294967296 | bytes 25165824 | tf_op jit(solution)/shard_map/rcnt,rcmt->cnm/dot_general | solution.py:82
  646.3 11.7 %fusion.44 = (bf16[1,16,8,64,16,16]{3,5,4,2,1,0:T(8,128)(2,1)}, bf16[1,16,8,64,16,16]{3,5,4,2,1,0:T(8,128)(2,1)}) fusion(bf16[2,16,8,64,16,16]{3,5,4,2,1,0:T(8,128)(2,1)} %bitcast.63), kind=kLoop, calls=%fused_computation.70 | loop fusion | flops 2097152 | bytes 16777216 | tf_op jit(solution)/shard_map/slice | solution.py:81
  658.0 20.2 %copy.64 = bf16[1,16,8,64,16,16]{3,2,5,4,1,0:T(8,128)(2,1)} copy(bf16[1,16,8,64,16,16]{3,5,4,2,1,0:T(8,128)(2,1)} %get-tuple-element.6) | data formatting | bytes 8388608 | tf_op jit(solution)/shard_map/neg | solution.py:81
  678.2 11.8 %neg.47 = bf16[1,16,512,256]{2,3,1,0:T(8,128)(2,1)} reshape(bf16[1,16,8,64,16,16]{3,2,5,4,1,0:T(8,128)(2,1)} %copy.64) | data formatting | bytes 8388608 | tf_op jit(solution)/shard_map/neg | solution.py:81
  690.1 6.3 copy.66
  696.4 20.2 %copy.63 = bf16[1,16,8,64,16,16]{3,2,5,4,1,0:T(8,128)(2,1)} copy(bf16[1,16,8,64,16,16]{3,5,4,2,1,0:T(8,128)(2,1)} %get-tuple-element.5) | data formatting | bytes 8388608 | tf_op jit(solution)/shard_map/slice | solution.py:81
  716.6 11.8 %slice.15 = bf16[1,16,512,256]{2,3,1,0:T(8,128)(2,1)} reshape(bf16[1,16,8,64,16,16]{3,2,5,4,1,0:T(8,128)(2,1)} %copy.63) | data formatting | bytes 8388608 | tf_op jit(solution)/shard_map/slice | solution.py:81
  728.4 6.3 copy.65
  734.8 62.4 %copy.68 = f32[16,512,512]{0,2,1:T(8,128)} copy(f32[16,512,512]{2,1,0:T(8,128)} %convolution_bitcast_fusion.1) | data formatting | bytes 33554432 | tf_op jit(solution)/shard_map/rcnt,rcmt->cnm/dot_general | solution.py:82
  797.1 5.5 gather_fusion
  802.8 69.5 %psum.7 = f32[512]{0:T(512)S(1)} all-reduce(f32[512]{0:T(512)S(1)} %reduce_sum.9), channel_id=1, replica_groups=mesh['stn'=8,'tm'=16] {'stn','tm'}, use_global_device_ids=true, to_apply=%region_1.2 | all-reduce | flops 512 | bytes 4096 | tf_op jit(solution)/shard_map/psum | solution.py:85
  872.5 18.9 %fusion.2 = f32[16,512,512]{2,1,0:T(8,128)} fusion(f32[16,512,512]{2,1,0:T(8,128)} %convolution_bitcast_fusion.1, bf16[1,16,512,256]{3,2,0,1:T(8,128)(2,1)} %copy.66, bf16[1,16,512,256]{3,2,0,1:T(8,128)(2,1)} %copy.65, bf16[2,16,512,256]{2,3,1,0:T(8,128)(2,1)} %reshape.236, f32[512,512]{1,0:T(8,128)S(1)} %multiply_multiply_fusion, ...), kind=kOutput, calls=%fused_computation.4 | convolution fusion | flops 4307550208 | bytes 51642368 | tf_op jit(solution)/shard_map/rcnt,rcmt->cnm/dot_general | solution.py:83
  (40 shorter events, 14.2 us)
Async XLA Ops:
  18.8 18.0 %copy-start.4 = (f32[16,4096]{1,0:T(8,128)S(1)}, f32[16,4096]{1,0:T(8,128)}, u32[]{:S(2)}) copy-start(f32[16,4096]{1,0:T(8,128)} %param.4) | copy-start | bytes 786436
  18.8 18.5 %copy-start.3 = (f32[64,2048]{1,0:T(8,128)S(1)}, f32[64,2048]{1,0:T(8,128)}, u32[]{:S(2)}) copy-start(f32[64,2048]{1,0:T(8,128)} %param.5) | copy-start | bytes 1572868
  18.8 95.6 %collective-permute-start = (bf16[64,15,4096]{2,0,1:T(8,128)(2,1)}, bf16[64,15,4096]{2,0,1:T(8,128)(2,1)}, u32[]{:S(2)}, u32[]{:S(2)}) collective-permute-start(bf16[64,15,4096]{2,0,1:T(8,128)(2,1)} %slice.19), channel_id=1, source_target_pairs={{0,1},{1,2},{2,3},{3,4},{4,5},{5,6},{6,7},{7,8},{8,9},{9,10},{10,1... | collective-permute-start | bytes 23592968 | tf_op jit(solution)/shard_map/ppermute | solution.py:12
  182.2 26.2 %copy-start.5 = (f32[1,64,64]{2,1,0:T(8,128)S(1)}, f32[1,64,64]{2,1,0:T(8,128)}, u32[]{:S(2)}) copy-start(f32[1,64,64]{2,1,0:T(8,128)} %get-tuple-element.15) | copy-start | bytes 49156
  182.2 26.2 %copy-start.6 = (f32[1,64,64]{2,1,0:T(8,128)S(1)}, f32[1,64,64]{2,1,0:T(8,128)}, u32[]{:S(2)}) copy-start(f32[1,64,64]{2,1,0:T(8,128)} %get-tuple-element.16) | copy-start | bytes 49156
  208.4 33.7 %copy-start.1 = (f32[2,32,64,2,64]{4,1,3,0,2:T(8,128)S(1)}, f32[2,32,64,2,64]{4,1,3,0,2:T(8,128)}, u32[]{:S(2)}) copy-start(f32[2,32,64,2,64]{4,1,3,0,2:T(8,128)} %copy.54) | copy-start | bytes 6291460
  208.4 96.9 %slice-start = ((s8[8388608]{0:T(1024)(128)(4,1)}), s8[4194304]{0:T(1024)(128)(4,1)S(1)}, s32[]{:S(2)}) async-start(s8[8388608]{0:T(1024)(128)(4,1)} %bitcast.66), calls=%async_computation.1 | async-start | bytes 8388608
  242.1 63.2 %slice-start.1 = ((s8[8388608]{0:T(1024)(128)(4,1)}), s8[4194304]{0:T(1024)(128)(4,1)S(1)}, s32[]{:S(2)}) async-start(s8[8388608]{0:T(1024)(128)(4,1)} %bitcast.66), calls=%async_computation.2 | async-start | bytes 8388608
  319.0 111.6 %all-to-all-start = ((bf16[2,128,16,1024]{3,2,0,1:T(8,128)(2,1)}), bf16[2,128,16,1024]{3,2,0,1:T(8,128)(2,1)}, u32[]{:S(2)}, u32[]{:S(2)}) async-start(bf16[2,128,16,1024]{3,2,0,1:T(8,128)(2,1)} %copy.57), calls=%async_computation | async-start | bytes 16777216 | tf_op jit(solution)/shard_map/all_to_all | solution.py:76
  734.8 62.4 %copy-start = (s32[512,1]{0,1:T(1,128)S(1)}, s32[512,1]{0,1:T(1,128)}, u32[]{:S(2)}) copy-start(s32[512,1]{0,1:T(1,128)} %shift-left_or_fusion) | copy-start | bytes 6148
  734.8 137.7 %copy-start.2 = (pred[512,512]{1,0:T(8,128)(4,1)S(1)}, pred[512,512]{1,0:T(8,128)(4,1)}, u32[]{:S(2)}) copy-start(pred[512,512]{1,0:T(8,128)(4,1)} %iota_compare_fusion) | copy-start | bytes 786436
where the time goes:
time: 907 us; the launch traced here: 892 us
  local copies, waits for them, and re-layouts  543 us (60%)
  matrix products  144 us (16%)
  waiting for transfers between devices  100 us (11%)
  blocking collectives  69.5 us (8%)
  other arithmetic  19.7 us (2%)
  starting transfers between devices  15.2 us (2%)
    reshape x2, local copies, waits for them, and re-layouts, per_device(): turned.reshape(2, station_groups, time_groups, per_group, inputs_dev, fra...  119 us
    all_to_all x1, waiting for transfers between devices, per_device(): lax.all_to_all(shaped, ('stn', 'tm'), split_axis=1, concat_axis=1, tiled=...  100 us
    mul x2, local copies, waits for them, and re-layouts, per_device(): spectrum.reshape(2, channels, inputs_dev, frames_dev)  76 us
    psum x1, blocking collectives, per_device(): power = lax.psum(local_power, ('stn', 'tm'))  69.5 us
    dot_general x1, local copies, waits for them, and re-layouts, per_device(): jnp.einsum('rcnt,rcmt->cnm', columns, columns, preferred_element_type=jnp...  62.4 us
    transpose x1, local copies, waits for them, and re-layouts, per_device(): jnp.transpose(blocks, (0, 3, 1, 4, 2, 5))  57.9 us
    reshape x2, local copies, waits for them, and re-layouts, transform(): arranged = filtered.reshape(row_count, outer_len, inner_len)  53.2 us
    dot_general x1, matrix products, transform(): jnp.einsum('qjksb,skbR->qjkR', combined, partial_ft, precision=highest)  47.6 us
  transfers between devices with their start and end apart: 2, of which 1 were waited for; matrix products, arithmetic and copies ran while one was open for 10% of the time, Pallas kernels for 0%

commit v1 on v0

v1 whole, which is shorter than its diff:
```python
import functools
import math

import jax
import jax.numpy as jnp
import numpy as np
from jax import lax
from jax.experimental import pallas as pl
from jax.experimental.pallas import tpu as pltpu
from jax.sharding import PartitionSpec as P

LANES = 128
RADIX = 32
SLOTS = 16
TAPS = 16
HALO = 8
PITCH = 32
GROUP = 8
Q_CHUNKS = (4, 4, 4, 4)
POWER_CHUNK = 1
INPUT_CHUNKS = 4


def real_dft(values):
    count = len(values)
    if count == 1:
        return [(values[0], None)]
    if count == 2:
        return [(values[0] + values[1], None), (values[0] - values[1], None)]
    even = real_dft(values[0::2])
    odd = real_dft(values[1::2])
    half, quarter = count // 2, count // 4
    bins = [None] * (half + 1)
    bins[0] = (even[0][0] + odd[0][0], None)
    bins[half] = (even[0][0] - odd[0][0], None)
    bins[quarter] = (even[quarter][0], -odd[quarter][0])
    for k in range(1, quarter):
        c, s = math.cos(2 * math.pi * k / count), math.sin(2 * math.pi * k / count)
        re, im = odd[k]
        if 8 * k == count:
            turned_re, turned_im = (re + im) * c, (im - re) * c
        else:
            turned_re, turned_im = re * c + im * s, im * c - re * s
        bins[k] = (even[k][0] + turned_re, even[k][1] + turned_im)
        bins[half - k] = (even[k][0] - turned_re, turned_im - even[k][1])
    return bins


def filter_body(flag_ref, own_ref, before_ref, after_ref, taps_ref, *rest):
    out_ref, frames_ref, filtered_ref = rest[-3:]
    tiles = own_ref.shape[2] // LANES
    frames = own_ref.shape[1]
    span = GROUP * PITCH
    flag = flag_ref[0]

    def widen(tile, carry):
        lanes = pl.ds(pl.multiple_of(tile * LANES, LANES), LANES)
        own = own_ref[:, :, lanes].astype(jnp.float32)
        before = before_ref[:, :, lanes].astype(jnp.float32)
        after = after_ref[:, :, lanes].astype(jnp.float32)
        for i in range(GROUP):
            row = pl.multiple_of(tile * span + i * PITCH, 8)
            frames_ref[pl.ds(row, HALO), :] = before[i]
            frames_ref[pl.ds(row + HALO, frames), :] = own[i]
            frames_ref[pl.ds(row + HALO + frames, HALO), :] = after[i]
        return carry

    lax.fori_loop(0, tiles, widen, 0)

    def fir(tile, carry):
        lanes = pl.ds(pl.multiple_of(tile * LANES, LANES), LANES)
        taps = [
            jnp.broadcast_to(taps_ref[p : p + 1, lanes], (GROUP, LANES)) for p in range(TAPS)
        ]
        for half in range(2):
            sums = [None] * HALO
            for r in range(1 + 8 * half, 24 + 8 * half):
                frame = frames_ref[pl.ds(tile * span + r, GROUP, stride=PITCH), :]
                if half == 1 and r < HALO + frames:
                    frame = frame * flag
                for j in range(HALO):
                    p = j + 8 * half + TAPS - r
                    if 0 <= p < TAPS:
                        term = taps[p] * frame
                        sums[j] = term if sums[j] is None else sums[j] + term
            for j in range(HALO):
                filtered_ref[j + 8 * half, tile] = sums[j]
        return carry

    lax.fori_loop(0, tiles, fir, 0)

    def butterfly(frame, carry):
        bins = real_dft([filtered_ref[frame, tile] for tile in range(tiles)])
        out_ref[0, frame, :, :LANES] = bins[0][0]
        out_ref[0, frame, :, LANES:] = bins[RADIX // 2][0]
        for q in range(1, SLOTS):
            out_ref[q, frame, :, :LANES] = bins[q][0]
            out_ref[q, frame, :, LANES:] = bins[q][1]
        return carry

    lax.fori_loop(0, frames, butterfly, 0)


def filter_call(flag, voltages, before, after, taps, partial, chunk):
    inputs, frames, length = voltages.shape
    groups = before.shape[0] // GROUP
    base = chunk * groups
    tiles = length // LANES
    operands = [flag, voltages, before, after, taps]
    in_specs = [
        pl.BlockSpec(memory_space=pltpu.SMEM),
        pl.BlockSpec((GROUP, frames, length), lambda g: (g + base, 0, 0)),
        pl.BlockSpec((GROUP, HALO, length), lambda g: (g, 0, 0)),
        pl.BlockSpec((GROUP, HALO, length), lambda g: (g, 0, 0)),
        pl.BlockSpec((TAPS, length), lambda g: (0, 0)),
    ]
    aliases = {}
    if partial is not None:
        operands.append(partial)
        in_specs.append(pl.BlockSpec(memory_space=pl.ANY))
        aliases = {5: 0}
    return pl.pallas_call(
        filter_body,
        name="filter",
        grid=(groups,),
        in_specs=in_specs,
        out_specs=pl.BlockSpec((SLOTS, frames, GROUP, 2 * LANES), lambda g: (0, 0, g + base, 0)),
        out_shape=jax.ShapeDtypeStruct((SLOTS, frames, inputs, 2 * LANES), jnp.float32),
        scratch_shapes=[
            pltpu.VMEM((tiles * GROUP * PITCH, LANES), jnp.float32),
            pltpu.VMEM((frames, tiles, GROUP, LANES), jnp.float32),
        ],
        input_output_aliases=aliases,
        compiler_params=pltpu.CompilerParams(vmem_limit_bytes=48 * 2**20),
    )(*operands)


def matmul_nt(left, right):
    return lax.dot_general(
        left, right, (((1,), (1,)), ((), ())), preferred_element_type=jnp.float32
    )


def split(value):
    high = value.astype(jnp.bfloat16)
    return high, (value - high.astype(jnp.float32)).astype(jnp.bfloat16)


def spectrum_body(
    first, part_ref, cos_ref, sin_ref, twist_cos_ref, twist_sin_ref, gain_ref, out_ref, power_ref, turn_ref
):
    step = pl.program_id(0)
    is_first = (step + first) == 0
    rows = part_ref.shape[1] * part_ref.shape[2]
    odd = lax.broadcasted_iota(jnp.int32, (LANES, LANES), 0) % 2 == 1
    twist_cos = jnp.where(odd, twist_cos_ref[0, 1:2, :], twist_cos_ref[0, 0:1, :])
    twist_sin = jnp.where(odd, twist_sin_ref[0, 1:2, :], twist_sin_ref[0, 0:1, :])
    cos = cos_ref[...] * twist_cos - sin_ref[...] * twist_sin
    sin = sin_ref[...] * twist_cos + cos_ref[...] * twist_sin
    special = jnp.where(is_first, 1.0, 0.0)
    drop = jnp.where(odd, special, 0.0)
    keep = 1.0 - drop
    sign = jnp.where(odd, -1.0, 1.0) * (1.0 - special)
    matrix = jnp.concatenate(
        [
            jnp.concatenate([cos * keep, sign * sin + drop * cos], axis=1),
            jnp.concatenate([-sin * keep, sign * cos - drop * sin], axis=1),
        ],
        axis=0,
    )
    matrix_high, matrix_low = split(matrix)
    part = part_ref[0].reshape(rows, 2 * LANES)
    gain = gain_ref[0]
    width = 2 * LANES
    for block in range(rows // width):
        part_high, part_low = split(part[block * width : (block + 1) * width])
        spec = (
            matmul_nt(matrix_high, part_high)
            + matmul_nt(matrix_high, part_low)
            + matmul_nt(matrix_low, part_high)
        )
        for side in range(2):
            for tile in range(width // LANES):
                value = spec[side * LANES : (side + 1) * LANES, tile * LANES : (tile + 1) * LANES]
                turn_ref[side, pl.ds(block * (width // LANES) + tile, LANES, stride=8), :] = (
                    value * gain
                )
    power = jnp.zeros((8, LANES), jnp.float32)
    for side in range(2):
        rounded = turn_ref[side].reshape(LANES, 8, LANES).astype(jnp.bfloat16)
        out_ref[:, side] = rounded
        wide = rounded.astype(jnp.float32)
        power = power + jnp.sum(wide * wide, axis=0)

    @pl.when(step == 0)
    def _():
        power_ref[...] = power

    @pl.when(step > 0)
    def _():
        power_ref[...] += power


def spectrum_call(partial, tables, gains, first, count, spare):
    _, frames, inputs, width = partial.shape
    cos, sin, twist_cos, twist_sin = tables
    whole = lambda q: (0, 0)
    pick = lambda q: (q + first, 0, 0)
    return pl.pallas_call(
        functools.partial(spectrum_body, first),
        name="spectrum",
        grid=(count,),
        in_specs=[
            pl.BlockSpec((1, frames, inputs, width), lambda q: (q + first, 0, 0, 0)),
            pl.BlockSpec((LANES, LANES), whole),
            pl.BlockSpec((LANES, LANES), whole),
            pl.BlockSpec((1, 2, LANES), pick),
            pl.BlockSpec((1, 2, LANES), pick),
            pl.BlockSpec((1, LANES, LANES), pick),
        ],
        out_specs=[
            pl.BlockSpec((LANES, 2, 8, LANES), lambda q: (0, q, 0, 0)),
            pl.BlockSpec((8, LANES), whole),
        ],
        out_shape=[
            jax.ShapeDtypeStruct((LANES, 2 * count + spare, 8, LANES), jnp.bfloat16),
            jax.ShapeDtypeStruct((8, LANES), jnp.float32),
        ],
        scratch_shapes=[pltpu.VMEM((2, 8 * LANES, LANES), jnp.float32)],
        compiler_params=pltpu.CompilerParams(vmem_limit_bytes=48 * 2**20),
    )(partial, cos, sin, twist_cos, twist_sin, gains)


def stamp_body(*refs):
    out_ref = refs[-1]
    total = refs[0][...]
    for ref in refs[1:-2]:
        total = total + ref[...]
    total = jnp.sum(total, axis=0, keepdims=True)
    high, rest = total.astype(jnp.bfloat16), total
    rest = rest - high.astype(jnp.float32)
    middle = rest.astype(jnp.bfloat16)
    low = (rest - middle.astype(jnp.float32)).astype(jnp.bfloat16)
    row = lax.broadcasted_iota(jnp.int32, (8, LANES), 0)
    tile = jnp.where(row == 0, high.astype(jnp.float32), 0.0)
    tile = jnp.where(row == 1, middle.astype(jnp.float32), tile)
    tile = jnp.where(row == 2, low.astype(jnp.float32), tile).astype(jnp.bfloat16)
    out_ref[...] = jnp.broadcast_to(tile[None, None], out_ref.shape)


def stamp_call(powers, payload):
    last = payload.shape[1] - 1
    return pl.pallas_call(
        stamp_body,
        name="stamp",
        grid=(1,),
        in_specs=[pl.BlockSpec((8, LANES), lambda i: (0, 0))] * len(powers)
        + [pl.BlockSpec(memory_space=pl.ANY)],
        out_specs=pl.BlockSpec((LANES, 1, 8, LANES), lambda i: (0, last, 0, 0)),
        out_shape=jax.ShapeDtypeStruct(payload.shape, payload.dtype),
        input_output_aliases={len(powers): 0},
    )(*powers, payload)


def correlate_body(groups, odd_ref, spec_ref, row_ref, col_ref, *rest):
    out_ref, left_ref, swapped_ref = rest[-3:]
    blocks = spec_ref.shape[0] // groups
    half = LANES // 2
    depth = blocks * 8
    for side in range(2):
        for s in range(groups):
            tile = spec_ref[s * blocks : (s + 1) * blocks, side].reshape(depth, LANES).T
            rows = slice(s * half, (s + 1) * half)
            for part in range(2):
                piece = tile[part * half : (part + 1) * half]
                at = part * depth
                left_ref[rows, side * 2 * depth + at : side * 2 * depth + at + depth] = piece
                other = (1 - side) * 2 * depth + at
                swapped_ref[rows, other : other + depth] = -piece if side == 0 else piece
    total = groups * half
    mid = total // 2
    for bi in range(2):
        for bj in range(2):
            rows, cols = slice(bi * mid, (bi + 1) * mid), slice(bj * mid, (bj + 1) * mid)
            weight = col_ref[rows, :] * row_ref[:, cols]
            right = left_ref[cols, :]
            if bi >= bj:
                real = matmul_nt(left_ref[rows, :], right)
            if bi <= bj:
                imag = matmul_nt(swapped_ref[rows, :], right)
            if bi == bj:
                lower = lax.broadcasted_iota(jnp.int32, (mid, mid), 0) >= lax.broadcasted_iota(
                    jnp.int32, (mid, mid), 1
                )
                value = jnp.where(lower, real, imag)
            else:
                value = real if bi > bj else imag
            out_ref[0, rows, cols] = value * weight


def correlate_call(odd, spectra, scale_row, scale_col, visibilities, first, count, groups, channels):
    total = scale_row.shape[1]
    place = lambda q, odd: (jnp.where(odd[0] == 1, (SLOTS - first - q) % SLOTS, first + q), 0, 0)
    operands = [odd, spectra, scale_row, scale_col]
    in_specs = [
        pl.BlockSpec((spectra.shape[0], 2, 8, LANES), lambda q, odd: (0, q, 0, 0)),
        pl.BlockSpec((1, total), lambda q, odd: (0, 0)),
        pl.BlockSpec((total, 1), lambda q, odd: (0, 0)),
    ]
    aliases = {}
    if visibilities is not None:
        operands.append(visibilities)
        in_specs.append(pl.BlockSpec(memory_space=pl.ANY))
        aliases = {4: 0}
    depth = 2 * spectra.shape[0] // groups * 16
    return pl.pallas_call(
        functools.partial(correlate_body, groups),
        name="correlate",
        grid_spec=pltpu.PrefetchScalarGridSpec(
            num_scalar_prefetch=1,
            grid=(count,),
            in_specs=in_specs,
            out_specs=pl.BlockSpec((1, total, total), place),
            scratch_shapes=[
                pltpu.VMEM((total, depth), jnp.bfloat16),
                pltpu.VMEM((total, depth), jnp.bfloat16),
            ],
        ),
        out_shape=jax.ShapeDtypeStruct((channels, total, total), jnp.float32),
        input_output_aliases=aliases,
        compiler_params=pltpu.CompilerParams(vmem_limit_bytes=48 * 2**20),
    )(*operands)


def trig_tables():
    dest = np.arange(LANES)[:, None]
    sample = np.arange(LANES)[None, :]
    angle = 2 * np.pi / 256 * ((dest * sample) % 256)
    offset = np.stack([np.arange(SLOTS), (SLOTS - np.arange(SLOTS)) % SLOTS], axis=1)
    twist = 2 * np.pi / 4096 * (offset[:, :, None] * np.arange(LANES)[None, None, :])
    tables = (np.cos(angle), np.sin(angle), np.cos(twist), np.sin(twist))
    return [jnp.asarray(table, jnp.float32) for table in tables]


def arrange_gains(gains):
    inputs, channels = gains.shape
    turned = gains.T.reshape(channels // (2 * SLOTS), 2, SLOTS, inputs)
    straight = turned[:, 0]
    reversed_ = jnp.roll(jnp.flip(turned[:, 1], axis=1), 1, axis=1)
    both = jnp.stack([straight, reversed_], axis=1).reshape(channels // SLOTS, SLOTS, inputs)
    by_slot = jnp.transpose(both, (1, 0, 2))
    return jnp.concatenate([by_slot, by_slot], axis=2)


def per_device(voltages, pfb_taps, eq_gains):
    inputs, frames, length = voltages.shape
    stations, times = lax.axis_size("stn"), lax.axis_size("tm")
    channels = eq_gains.shape[1]
    here = lax.axis_index("tm")
    forward = [(i, i + 1) for i in range(times - 1)]
    backward = [((i + 1) % times, i) for i in range(times)]
    flag = jnp.where(here == times - 1, 0.0, 1.0).astype(jnp.float32).reshape(1)
    size = inputs // INPUT_CHUNKS
    halos = []
    for chunk in range(INPUT_CHUNKS):
        block = voltages[chunk * size : (chunk + 1) * size]
        halos.append(
            (
                lax.ppermute(block[:, frames - HALO :], "tm", forward),
                lax.ppermute(block[:, :HALO], "tm", backward),
            )
        )
    gains = arrange_gains(eq_gains)
    tables = trig_tables()
    partial = None
    for chunk in range(INPUT_CHUNKS):
        before, after = halos[chunk]
        partial = filter_call(flag, voltages, before, after, pfb_taps, partial, chunk)
    payloads, powers, first = [], [], 0
    for index, count in enumerate(Q_CHUNKS):
        spare = 1 if index == POWER_CHUNK else 0
        payload, power = spectrum_call(partial, tables, gains, first, count, spare)
        payloads.append(payload)
        powers.append(power)
        first += count
    payloads[POWER_CHUNK] = stamp_call(powers, payloads[POWER_CHUNK])
    received = [
        lax.all_to_all(payload, ("stn", "tm"), split_axis=0, concat_axis=0, tiled=True)
        for payload in payloads
    ]
    parts = received[POWER_CHUNK][:, 2 * Q_CHUNKS[POWER_CHUNK], :3].astype(jnp.float32)
    parts = parts.reshape(stations, times, 3, LANES // inputs, inputs)
    power = jnp.sum(parts, axis=(1, 2, 3)).reshape(stations * inputs)
    all_frames = frames * times
    scale = lax.rsqrt(power / (all_frames * channels) + 1e-06)
    scale_row = (scale / all_frames).reshape(1, -1)
    scale_col = scale.reshape(-1, 1)
    odd = (here % 2).astype(jnp.int32).reshape(1)
    visibilities, first = None, 0
    for index, count in enumerate(Q_CHUNKS):
        visibilities = correlate_call(
            odd,
            received[index],
            scale_row,
            scale_col,
            visibilities,
            first,
            count,
            stations,
            channels // (stations * times),
        )
        first += count
    return visibilities


def solution(mesh):
    in_specs = (P("stn", "tm", None), P(), P("stn", None))
    out_specs = P(("stn", "tm"), None, None)
    return jax.shard_map(
        per_device, mesh=mesh, in_specs=in_specs, out_specs=out_specs, check_vma=False
    )
```

time: 907 us -> 267 us (0.29); the launches traced: 892 us -> 266 us
  local copies, waits for them, and re-layouts: 543 us -> 25.2 us
  matrix products: 144 us -> 0 us
  Pallas kernels: 0 us -> 93.9 us
  blocking collectives: 69.5 us -> 37.7 us
  waiting for transfers between devices: 100 us -> 68.3 us
  starting transfers between devices: 15.2 us -> 36.3 us
  other arithmetic: 19.7 us -> 4.36 us
    reshape x5 -> x0, local copies, waits for them, and re-layouts: 195 us -> none  [the longest x2 119 us: per_device(): turned.reshape(2, station_groups, time_groups, per_group, inputs_dev, fra...]
    dot_general x5 -> x0, matrix products: 122 us -> none  [the longest x1 47.6 us: transform(): jnp.einsum('qjksb,skbR->qjkR', combined, partial_ft, precision=highest)]
    pallas_call x0 -> x13, Pallas kernels: none -> 93.9 us  [the longest x4 51.2 us: filter_call(): pl.pallas_call(filter_body, name='filter', grid=(groups,), in_specs=in_sp...]
    transpose x4 -> x0, local copies, waits for them, and re-layouts: 80.7 us -> none  [the longest x1 57.9 us: per_device(): jnp.transpose(blocks, (0, 3, 1, 4, 2, 5))]
    mul x2 -> x0, local copies, waits for them, and re-layouts: 76 us -> none  [per_device(): spectrum.reshape(2, channels, inputs_dev, frames_dev)]
    psum x1 -> x0, blocking collectives: 69.5 us -> none  [per_device(): power = lax.psum(local_power, ('stn', 'tm'))]
    dot_general x1 -> x0, local copies, waits for them, and re-layouts: 62.4 us -> none  [per_device(): jnp.einsum('rcnt,rcmt->cnm', columns, columns, preferred_element_type=jnp...]
    all_to_all x1 -> x3, waiting for transfers between devices: 100 us -> 53.7 us  [per_device(): lax.all_to_all(payload, ('stn', 'tm'), split_axis=0, concat_axis=0, tiled...]
  transfers between devices with their start and end apart: 2 -> 11, of which waited for: 1 -> 5; matrix products, arithmetic and copies ran while one was open for 10% -> 5% of each run, Pallas kernels for 0% -> 26%
where the time goes in v1:
time: 267 us; the launch traced here: 266 us
  Pallas kernels  93.9 us (35%)
  waiting for transfers between devices  68.3 us (26%)
  blocking collectives  37.7 us (14%)
  starting transfers between devices  36.3 us (14%)
  local copies, waits for them, and re-layouts  25.2 us (9%)
  other arithmetic  4.36 us (2%)
    all_to_all x3, waiting for transfers between devices, per_device(): lax.all_to_all(payload, ('stn', 'tm'), split_axis=0, concat_axis=0, tiled...  53.7 us
    pallas_call x4, Pallas kernels, filter_call(): pl.pallas_call(filter_body, name='filter', grid=(groups,), in_specs=in_sp...  51.2 us
    all_to_all x1, blocking collectives, per_device(): lax.all_to_all(payload, ('stn', 'tm'), split_axis=0, concat_axis=0, tiled...  37.7 us
    all_to_all x3, starting transfers between devices, per_device(): lax.all_to_all(payload, ('stn', 'tm'), split_axis=0, concat_axis=0, tiled...  22.9 us
    pallas_call x4, Pallas kernels, spectrum_call(): pl.pallas_call(functools.partial(spectrum_body, first), name='spectrum',...  21.3 us
    pallas_call x4, Pallas kernels, correlate_call(): pl.pallas_call(functools.partial(correlate_body, groups), name='correlate...  19.9 us
    ppermute x4, waiting for transfers between devices, per_device(): lax.ppermute(block[:, frames - HALO:], 'tm', forward)  14.6 us
    unnamed x42, local copies, waits for them, and re-layouts  14.6 us
  transfers between devices with their start and end apart: 11, of which 5 were waited for; matrix products, arithmetic and copies ran while one was open for 5% of the time, Pallas kernels for 26%

profile of v1, /device:TPU:1, one launch (start us, length us, event | category | flops | bytes accessed | tf_op | source)
XLA Modules:
  0.0 266.0 jit_solution(17696011755411533137)
XLA Ops:
  0.0 5.6 %fusion = (bf16[16,8,4096]{2,1,0:T(8,128)(2,1)S(1)}, bf16[16,8,4096]{2,1,0:T(8,128)(2,1)S(1)}, bf16[16,8,4096]{2,1,0:T(8,128)(2,1)}, bf16[16,8,4096]{2,1,0:T(8,1...) fusion(bf16[64,16,4096]{2,1,0:T(8,128)(2,1)} %own_ref.7), kind=kLoop, calls=%fused_computation.8 | loop fusion | bytes 16777216 | tf_op jit(solution)/shard_map/slice | solution.py:370
  5.7 5.1 %collective-permute-start.4 = (bf16[16,8,4096]{2,1,0:T(8,128)(2,1)S(1)}, bf16[16,8,4096]{2,1,0:T(8,128)(2,1)S(1)}, u32[]{:S(2)}, u32[]{:S(2)}) collective-permute-start(bf16[16,8,4096]{2,1,0:T(8,128)(2,1)S(1)} %get-tuple-element.24), channel_id=1, source_target_pairs={{0,1},{1,2},{2,3},{3,4},{4,5},{5,6},{6,7},{7,8},{8,9},{9,10},{10,1... | collective-permute-start | bytes 3145736 | tf_op jit(solution)/shard_map/ppermute | solution.py:369
  10.7 1.9 collective-permute-start.6
  13.3 3.4 %collective-permute-start = (bf16[16,8,4096]{2,1,0:T(8,128)(2,1)}, bf16[16,8,4096]{2,1,0:T(8,128)(2,1)S(1)}, u32[]{:S(2)}, u32[]{:S(2)}) collective-permute-start(bf16[16,8,4096]{2,1,0:T(8,128)(2,1)} %get-tuple-element.28), channel_id=1, source_target_pairs={{0,1},{1,2},{2,3},{3,4},{4,5},{5,6},{6,7},{7,8},{8,9},{9,10},{10,1... | collective-permute-start | bytes 3145736 | tf_op jit(solution)/shard_map/ppermute | solution.py:369
  16.7 2.4 collective-permute-start.2
  19.1 3.4 %collective-permute-done.4.before_ref = bf16[16,8,4096]{2,1,0:T(8,128)(2,1)S(1)} collective-permute-done((bf16[16,8,4096]{2,1,0:T(8,128)(2,1)S(1)}, bf16[16,8,4096]{2,1,0:T(8,128)(2,1)S(1)}, u32[]{:S(2)}, u32[]{:S(2)}) %collective-permute-start.4) | collective-permute-done | bytes 1048608 | tf_op jit(solution)/shard_map/ppermute | solution.py:369
  22.5 11.2 %collective-permute-done.6.before_ref = bf16[16,8,4096]{2,1,0:T(8,128)(2,1)S(1)} collective-permute-done((bf16[16,8,4096]{2,1,0:T(8,128)(2,1)S(1)}, bf16[16,8,4096]{2,1,0:T(8,128)(2,1)S(1)}, u32[]{:S(2)}, u32[]{:S(2)}) %collective-permute-start.6) | collective-permute-done | bytes 1048608 | tf_op jit(solution)/shard_map/ppermute | solution.py:369
  34.7 2.3 copy.31
  37.1 2.1 slice_bitcast_fusion.1
  40.0 1.9 slice.69
  44.2 1.8 copy.33
  46.0 1.9 pad_maximum_fusion.1.gain_ref
  50.3 12.6 %filter.4.rest_0_ = f32[16,16,64,256]{3,2,1,0:T(8,128)} custom-call(f32[1]{0:T(128)} %bitcast.1.flag_ref, bf16[64,16,4096]{2,1,0:T(8,128)(2,1)} %own_ref.7, bf16[16,8,4096]{2,1,0:T(8,128)(2,1)S(1)} %copy-done.10, bf16[16,8,4096]{2,1,0:T(8,128)(2,1)S(1)} %copy-done.12, f32[16,4096]{1,0:T(8,128)S(1)} %copy-done.3), custom_call_target="tpu_custom_call" | custom-call | tf_op jit(solution)/shard_map/filter/pallas_call | solution.py:122
  63.0 12.8 %filter.5.rest_0_ = f32[16,16,64,256]{3,2,1,0:T(8,128)} custom-call(f32[1]{0:T(128)} %bitcast.1.flag_ref, bf16[64,16,4096]{2,1,0:T(8,128)(2,1)} %own_ref.7, bf16[16,8,4096]{2,1,0:T(8,128)(2,1)S(1)} %collective-permute-done.4.before_ref, bf16[16,8,4096]{2,1,0:T(8,128)(2,1)} %collective-permute-done.5.after_ref, ...), custom_call_target="tpu_custom_call", output_to_operand_aliasing={{}: (5, {})} | custom-call | tf_op jit(solution)/shard_map/filter/pallas_call | solution.py:122
  75.8 13.0 %filter.6.rest_0_ = f32[16,16,64,256]{3,2,1,0:T(8,128)} custom-call(f32[1]{0:T(128)} %bitcast.1.flag_ref, bf16[64,16,4096]{2,1,0:T(8,128)(2,1)} %own_ref.7, bf16[16,8,4096]{2,1,0:T(8,128)(2,1)} %collective-permute-done.2.before_ref, bf16[16,8,4096]{2,1,0:T(8,128)(2,1)} %collective-permute-done.3.after_ref, ...), custom_call_target="tpu_custom_call", output_to_operand_aliasing={{}: (5, {})} | custom-call | tf_op jit(solution)/shard_map/filter/pallas_call | solution.py:122
  88.8 12.8 %filter.7.part_ref = f32[16,16,64,256]{3,2,1,0:T(8,128)} custom-call(f32[1]{0:T(128)} %bitcast.1.flag_ref, bf16[64,16,4096]{2,1,0:T(8,128)(2,1)} %own_ref.7, bf16[16,8,4096]{2,1,0:T(8,128)(2,1)S(1)} %collective-permute-done.before_ref, bf16[16,8,4096]{2,1,0:T(8,128)(2,1)} %collective-permute-done.1.after_ref, ...), custom_call_target="tpu_custom_call", output_to_operand_aliasing={{}: (5, {})} | custom-call | tf_op jit(solution)/shard_map/filter/pallas_call | solution.py:122
  101.6 5.3 %spectrum.7 = (bf16[128,8,8,128]{3,2,1,0:T(8,128)(2,1)S(1)}, f32[8,128]{1,0:T(8,128)S(1)}) custom-call(f32[16,16,64,256]{3,2,1,0:T(8,128)} %filter.7.part_ref, f32[128,128]{1,0:T(8,128)S(1)} %copy-done.7, f32[128,128]{1,0:T(8,128)S(1)} %copy-done.8, f32[16,2,128]{2,1,0:T(2,128)S(1)} %copy-done.13, f32[16,2,128]{2,1,0:T(2,128)S(1)} %copy-done.14, ...), custom_call_target="tpu_custom_call" | custom-call | tf_op jit(solution)/shard_map/spectrum/pallas_call | solution.py:209
  108.9 12.2 %all-to-all-start.2 = ((bf16[128,8,8,128]{3,2,1,0:T(8,128)(2,1)}), bf16[128,8,8,128]{3,2,1,0:T(8,128)(2,1)S(1)}, u32[]{:S(2)}, u32[]{:S(2)}) async-start(bf16[128,8,8,128]{3,2,1,0:T(8,128)(2,1)} %copy-done.6), calls=%async_computation.2 | async-start | bytes 4194304 | tf_op jit(solution)/shard_map/all_to_all | solution.py:388
  121.1 5.3 %spectrum.5 = (bf16[128,8,8,128]{3,2,1,0:T(8,128)(2,1)S(1)}, f32[8,128]{1,0:T(8,128)S(1)}) custom-call(f32[16,16,64,256]{3,2,1,0:T(8,128)} %filter.7.part_ref, f32[128,128]{1,0:T(8,128)S(1)} %copy-done.7, f32[128,128]{1,0:T(8,128)S(1)} %copy-done.8, f32[16,2,128]{2,1,0:T(2,128)S(1)} %copy-done.13, f32[16,2,128]{2,1,0:T(2,128)S(1)} %copy-done.15, ...), custom_call_target="tpu_custom_call" | custom-call | tf_op jit(solution)/shard_map/spectrum/pallas_call | solution.py:209
  127.8 23.7 %all-to-all-done.2.spec_ref = bf16[128,8,8,128]{3,2,1,0:T(8,128)(2,1)S(1)} async-done(((bf16[128,8,8,128]{3,2,1,0:T(8,128)(2,1)}), bf16[128,8,8,128]{3,2,1,0:T(8,128)(2,1)S(1)}, u32[]{:S(2)}, u32[]{:S(2)}) %all-to-all-start.2) | async-done | bytes 2097184 | tf_op jit(solution)/shard_map/all_to_all | solution.py:388
  151.6 5.3 %all-to-all-start.3 = ((bf16[128,8,8,128]{3,2,1,0:T(8,128)(2,1)}), bf16[128,8,8,128]{3,2,1,0:T(8,128)(2,1)}, u32[]{:S(2)}, u32[]{:S(2)}) async-start(bf16[128,8,8,128]{3,2,1,0:T(8,128)(2,1)} %copy-done.5), calls=%async_computation.3 | async-start | bytes 4194304 | tf_op jit(solution)/shard_map/all_to_all | solution.py:388
  156.9 5.3 %spectrum.4 = (bf16[128,8,8,128]{3,2,1,0:T(8,128)(2,1)S(1)}, f32[8,128]{1,0:T(8,128)S(1)}) custom-call(f32[16,16,64,256]{3,2,1,0:T(8,128)} %filter.7.part_ref, f32[128,128]{1,0:T(8,128)S(1)} %copy-done.7, f32[128,128]{1,0:T(8,128)S(1)} %copy-done.8, f32[16,2,128]{2,1,0:T(2,128)S(1)} %copy-done.13, f32[16,2,128]{2,1,0:T(2,128)S(1)} %copy-done.15, ...), custom_call_target="tpu_custom_call" | custom-call | tf_op jit(solution)/shard_map/spectrum/pallas_call | solution.py:209
  163.6 5.4 %spectrum.6 = (bf16[128,9,8,128]{3,2,1,0:T(8,128)(2,1)S(1)}, f32[8,128]{1,0:T(8,128)S(1)}) custom-call(f32[16,16,64,256]{3,2,1,0:T(8,128)} %filter.7.part_ref, f32[128,128]{1,0:T(8,128)S(1)} %copy-done.7, f32[128,128]{1,0:T(8,128)S(1)} %copy-done.8, f32[16,2,128]{2,1,0:T(2,128)S(1)} %copy-done.13, f32[16,2,128]{2,1,0:T(2,128)S(1)} %copy-done.15, ...), custom_call_target="tpu_custom_call" | custom-call | tf_op jit(solution)/shard_map/spectrum/pallas_call | solution.py:209
  171.0 1.4 stamp.1
  172.4 14.7 %all-to-all-done.3.spec_ref = bf16[128,8,8,128]{3,2,1,0:T(8,128)(2,1)} async-done(((bf16[128,8,8,128]{3,2,1,0:T(8,128)(2,1)}), bf16[128,8,8,128]{3,2,1,0:T(8,128)(2,1)}, u32[]{:S(2)}, u32[]{:S(2)}) %all-to-all-start.3) | async-done | bytes 2097184 | tf_op jit(solution)/shard_map/all_to_all | solution.py:388
  187.1 37.7 %all_to_all.20.spec_ref = bf16[128,9,8,128]{3,2,1,0:T(8,128)(2,1)S(1)} all-to-all(bf16[128,9,8,128]{3,2,1,0:T(8,128)(2,1)} %stamp.1), channel_id=1, replica_groups=mesh['stn'=8,'tm'=16] {'stn','tm'}, dimensions={0} | all-to-all | bytes 4718592 | tf_op jit(solution)/shard_map/all_to_all | solution.py:388
  224.8 5.4 %all-to-all-start = ((bf16[128,8,8,128]{3,2,1,0:T(8,128)(2,1)}), bf16[128,8,8,128]{3,2,1,0:T(8,128)(2,1)}, u32[]{:S(2)}, u32[]{:S(2)}) async-start(bf16[128,8,8,128]{3,2,1,0:T(8,128)(2,1)} %copy-done.4), calls=%async_computation | async-start | bytes 4194304 | tf_op jit(solution)/shard_map/all_to_all | solution.py:388
  230.9 5.6 %correlate.4.rest_0_ = f32[16,512,512]{2,1,0:T(8,128)} custom-call(s32[1]{0:T(128)} %bitcast.odd_ref, bf16[128,8,8,128]{3,2,1,0:T(8,128)(2,1)} %all-to-all-done.3.spec_ref, f32[1,512]{1,0:T(1,128)S(1)} %div.18.row_ref, f32[512,1]{1,0:T(8,128)S(1)} %rsqrt.23.col_ref), custom_call_target="tpu_custom_call" | custom-call | tf_op jit(solution)/shard_map/correlate/pallas_call | solution.py:316
  236.5 4.4 %correlate.5.rest_0_ = f32[16,512,512]{2,1,0:T(8,128)} custom-call(s32[1]{0:T(128)} %bitcast.odd_ref, bf16[128,9,8,128]{3,2,1,0:T(8,128)(2,1)S(1)} %all_to_all.20.spec_ref, f32[1,512]{1,0:T(1,128)S(1)} %div.18.row_ref, f32[512,1]{1,0:T(8,128)S(1)} %rsqrt.23.col_ref, f32[16,512,512]{2,1,0:T(8,128)} %correlate.4.rest_0_), custom_call_target="tpu_custom_call", output_to_operand_aliasing={{}: (4, {})} | custom-call | tf_op jit(solution)/shard_map/correlate/pallas_call | solution.py:316
  240.9 4.3 %correlate.6.rest_0_ = f32[16,512,512]{2,1,0:T(8,128)} custom-call(s32[1]{0:T(128)} %bitcast.odd_ref, bf16[128,8,8,128]{3,2,1,0:T(8,128)(2,1)S(1)} %copy-done.2, f32[1,512]{1,0:T(1,128)S(1)} %div.18.row_ref, f32[512,1]{1,0:T(8,128)S(1)} %rsqrt.23.col_ref, f32[16,512,512]{2,1,0:T(8,128)} %correlate.5.rest_0_), custom_call_target="tpu_custom_call", output_to_operand_aliasing={{}: (4, {})} | custom-call | tf_op jit(solution)/shard_map/correlate/pallas_call | solution.py:316
  245.2 15.2 %all-to-all-done.spec_ref = bf16[128,8,8,128]{3,2,1,0:T(8,128)(2,1)} async-done(((bf16[128,8,8,128]{3,2,1,0:T(8,128)(2,1)}), bf16[128,8,8,128]{3,2,1,0:T(8,128)(2,1)}, u32[]{:S(2)}, u32[]{:S(2)}) %all-to-all-start) | async-done | bytes 2097184 | tf_op jit(solution)/shard_map/all_to_all | solution.py:388
  260.4 5.6 %correlate.7 = f32[16,512,512]{2,1,0:T(8,128)} custom-call(s32[1]{0:T(128)} %bitcast.odd_ref, bf16[128,8,8,128]{3,2,1,0:T(8,128)(2,1)} %all-to-all-done.spec_ref, f32[1,512]{1,0:T(1,128)S(1)} %div.18.row_ref, f32[512,1]{1,0:T(8,128)S(1)} %rsqrt.23.col_ref, f32[16,512,512]{2,1,0:T(8,128)} %correlate.6.rest_0_), custom_call_target="tpu_custom_call", output_to_operand_aliasing={{}: (4, {})} | custom-call | tf_op jit(solution)/shard_map/correlate/pallas_call | solution.py:316
  (60 shorter events, 14.5 us)
Async XLA Ops:
  5.7 42.2 %copy-start.3 = (f32[16,4096]{1,0:T(8,128)S(1)}, f32[16,4096]{1,0:T(8,128)}, u32[]{:S(2)}) copy-start(f32[16,4096]{1,0:T(8,128)} %taps_ref.7) | copy-start | bytes 786436
  5.7 16.8 %collective-permute-start.4 = (bf16[16,8,4096]{2,1,0:T(8,128)(2,1)S(1)}, bf16[16,8,4096]{2,1,0:T(8,128)(2,1)S(1)}, u32[]{:S(2)}, u32[]{:S(2)}) collective-permute-start(bf16[16,8,4096]{2,1,0:T(8,128)(2,1)S(1)} %get-tuple-element.24), channel_id=1, source_target_pairs={{0,1},{1,2},{2,3},{3,4},{4,5},{5,6},{6,7},{7,8},{8,9},{9,10},{10,1... | collective-permute-start | bytes 3145736 | tf_op jit(solution)/shard_map/ppermute | solution.py:369
  10.7 23.0 %collective-permute-start.6 = (bf16[16,8,4096]{2,1,0:T(8,128)(2,1)S(1)}, bf16[16,8,4096]{2,1,0:T(8,128)(2,1)S(1)}, u32[]{:S(2)}, u32[]{:S(2)}) collective-permute-start(bf16[16,8,4096]{2,1,0:T(8,128)(2,1)S(1)} %get-tuple-element.22), channel_id=1, source_target_pairs={{0,1},{1,2},{2,3},{3,4},{4,5},{5,6},{6,7},{7,8},{8,9},{9,10},{10,1... | collective-permute-start | bytes 3145736 | tf_op jit(solution)/shard_map/ppermute | solution.py:369
  12.7 21.0 %collective-permute-start.7 = (bf16[16,8,4096]{2,1,0:T(8,128)(2,1)S(1)}, bf16[16,8,4096]{2,1,0:T(8,128)(2,1)S(1)}, u32[]{:S(2)}, u32[]{:S(2)}) collective-permute-start(bf16[16,8,4096]{2,1,0:T(8,128)(2,1)S(1)} %get-tuple-element.21), channel_id=1, source_target_pairs={{1,0},{2,1},{3,2},{4,3},{5,4},{6,5},{7,6},{8,7},{9,8},{10,9},{11,1... | collective-permute-start | bytes 3145736 | tf_op jit(solution)/shard_map/ppermute | solution.py:370
  13.3 75.5 %collective-permute-start = (bf16[16,8,4096]{2,1,0:T(8,128)(2,1)}, bf16[16,8,4096]{2,1,0:T(8,128)(2,1)S(1)}, u32[]{:S(2)}, u32[]{:S(2)}) collective-permute-start(bf16[16,8,4096]{2,1,0:T(8,128)(2,1)} %get-tuple-element.28), channel_id=1, source_target_pairs={{0,1},{1,2},{2,3},{3,4},{4,5},{5,6},{6,7},{7,8},{8,9},{9,10},{10,1... | collective-permute-start | bytes 3145736 | tf_op jit(solution)/shard_map/ppermute | solution.py:369
  16.7 59.1 %collective-permute-start.2 = (bf16[16,8,4096]{2,1,0:T(8,128)(2,1)}, bf16[16,8,4096]{2,1,0:T(8,128)(2,1)}, u32[]{:S(2)}, u32[]{:S(2)}) collective-permute-start(bf16[16,8,4096]{2,1,0:T(8,128)(2,1)} %get-tuple-element.26), channel_id=1, source_target_pairs={{0,1},{1,2},{2,3},{3,4},{4,5},{5,6},{6,7},{7,8},{8,9},{9,10},{10,1... | collective-permute-start | bytes 3145736 | tf_op jit(solution)/shard_map/ppermute | solution.py:369
  22.5 40.5 %collective-permute-start.5 = (bf16[16,8,4096]{2,1,0:T(8,128)(2,1)}, bf16[16,8,4096]{2,1,0:T(8,128)(2,1)}, u32[]{:S(2)}, u32[]{:S(2)}) collective-permute-start(bf16[16,8,4096]{2,1,0:T(8,128)(2,1)} %get-tuple-element.23), channel_id=1, source_target_pairs={{1,0},{2,1},{3,2},{4,3},{5,4},{6,5},{7,6},{8,7},{9,8},{10,9},{11,1... | collective-permute-start | bytes 3145736 | tf_op jit(solution)/shard_map/ppermute | solution.py:370
  33.7 12.3 %copy-start.9 = (bf16[16,8,4096]{2,1,0:T(8,128)(2,1)}, bf16[16,8,4096]{2,1,0:T(8,128)(2,1)S(1)}, u32[]{:S(2)}) copy-start(bf16[16,8,4096]{2,1,0:T(8,128)(2,1)S(1)} %collective-permute-done.6.before_ref) | copy-start | bytes 3145732
  33.7 42.1 %collective-permute-start.3 = (bf16[16,8,4096]{2,1,0:T(8,128)(2,1)}, bf16[16,8,4096]{2,1,0:T(8,128)(2,1)}, u32[]{:S(2)}, u32[]{:S(2)}) collective-permute-start(bf16[16,8,4096]{2,1,0:T(8,128)(2,1)} %get-tuple-element.25), channel_id=1, source_target_pairs={{1,0},{2,1},{3,2},{4,3},{5,4},{6,5},{7,6},{8,7},{9,8},{10,9},{11,1... | collective-permute-start | bytes 3145736 | tf_op jit(solution)/shard_map/ppermute | solution.py:370
  33.7 1.0 copy-start.11
  34.7 54.0 %collective-permute-start.1 = (bf16[16,8,4096]{2,1,0:T(8,128)(2,1)}, bf16[16,8,4096]{2,1,0:T(8,128)(2,1)}, u32[]{:S(2)}, u32[]{:S(2)}) collective-permute-start(bf16[16,8,4096]{2,1,0:T(8,128)(2,1)} %get-tuple-element.27), channel_id=1, source_target_pairs={{1,0},{2,1},{3,2},{4,3},{5,4},{6,5},{7,6},{8,7},{9,8},{10,9},{11,1... | collective-permute-start | bytes 3145736 | tf_op jit(solution)/shard_map/ppermute | solution.py:370
  47.9 1.2 copy-start.10
  49.1 1.2 copy-start.12
  88.7 12.9 %copy-start.7 = (f32[128,128]{1,0:T(8,128)S(1)}, f32[128,128]{1,0:T(8,128)}, u32[]{:S(2)}) copy-start(f32[128,128]{1,0:T(8,128)} %constant.39.clone.cos_ref) | copy-start | bytes 196612
  88.7 12.9 %copy-start.8 = (f32[128,128]{1,0:T(8,128)S(1)}, f32[128,128]{1,0:T(8,128)}, u32[]{:S(2)}) copy-start(f32[128,128]{1,0:T(8,128)} %constant.40.clone.sin_ref) | copy-start | bytes 196612
  88.7 12.9 %copy-start.13 = (f32[16,2,128]{2,1,0:T(2,128)S(1)}, f32[16,2,128]{2,1,0:T(2,128)}, u32[]{:S(2)}) copy-start(f32[16,2,128]{2,1,0:T(2,128)} %constant.41.clone.twist_cos_ref) | copy-start | bytes 49156
  88.8 12.9 %copy-start.14 = (f32[16,2,128]{2,1,0:T(2,128)S(1)}, f32[16,2,128]{2,1,0:T(2,128)}, u32[]{:S(2)}) copy-start(f32[16,2,128]{2,1,0:T(2,128)} %constant.42.clone.twist_sin_ref) | copy-start | bytes 49156
  101.6 19.5 %copy-start.15 = (f32[16,2,128]{2,1,0:T(2,128)S(1)}, f32[16,2,128]{2,1,0:T(2,128)}, u32[]{:S(2)}) copy-start(f32[16,2,128]{2,1,0:T(2,128)} %constant.42.clone.twist_sin_ref) | copy-start | bytes 49156
  107.0 1.3 copy-start.6
  108.3 0.6 copy-start.16
  108.9 42.7 %all-to-all-start.2 = ((bf16[128,8,8,128]{3,2,1,0:T(8,128)(2,1)}), bf16[128,8,8,128]{3,2,1,0:T(8,128)(2,1)S(1)}, u32[]{:S(2)}, u32[]{:S(2)}) async-start(bf16[128,8,8,128]{3,2,1,0:T(8,128)(2,1)} %copy-done.6), calls=%async_computation.2 | async-start | bytes 4194304 | tf_op jit(solution)/shard_map/all_to_all | solution.py:388
  126.4 1.4 copy-start.5
  127.8 34.4 %copy-start.17 = (f32[8,128]{1,0:T(8,128)}, f32[8,128]{1,0:T(8,128)S(1)}, u32[]{:S(2)}) copy-start(f32[8,128]{1,0:T(8,128)S(1)} %get-tuple-element.14.refs_0_) | copy-start | bytes 12292
  151.6 10.6 %copy-start.1 = (bf16[128,8,8,128]{3,2,1,0:T(8,128)(2,1)}, bf16[128,8,8,128]{3,2,1,0:T(8,128)(2,1)S(1)}, u32[]{:S(2)}) copy-start(bf16[128,8,8,128]{3,2,1,0:T(8,128)(2,1)S(1)} %all-to-all-done.2.spec_ref) | copy-start | bytes 6291460
  151.6 35.5 %all-to-all-start.3 = ((bf16[128,8,8,128]{3,2,1,0:T(8,128)(2,1)}), bf16[128,8,8,128]{3,2,1,0:T(8,128)(2,1)}, u32[]{:S(2)}, u32[]{:S(2)}) async-start(bf16[128,8,8,128]{3,2,1,0:T(8,128)(2,1)} %copy-done.5), calls=%async_computation.3 | async-start | bytes 4194304 | tf_op jit(solution)/shard_map/all_to_all | solution.py:388
  162.2 1.3 copy-start.4
  163.5 5.4 %copy-start.18 = (f32[8,128]{1,0:T(8,128)}, f32[8,128]{1,0:T(8,128)S(1)}, u32[]{:S(2)}) copy-start(f32[8,128]{1,0:T(8,128)S(1)} %get-tuple-element.17.refs_3_) | copy-start | bytes 12292
  169.0 1.4 copy-start
  170.4 0.6 copy-start.19
  224.8 35.6 %all-to-all-start = ((bf16[128,8,8,128]{3,2,1,0:T(8,128)(2,1)}), bf16[128,8,8,128]{3,2,1,0:T(8,128)(2,1)}, u32[]{:S(2)}, u32[]{:S(2)}) async-start(bf16[128,8,8,128]{3,2,1,0:T(8,128)(2,1)} %copy-done.4), calls=%async_computation | async-start | bytes 4194304 | tf_op jit(solution)/shard_map/all_to_all | solution.py:388
  236.5 4.4 %copy-start.2 = (bf16[128,8,8,128]{3,2,1,0:T(8,128)(2,1)S(1)}, bf16[128,8,8,128]{3,2,1,0:T(8,128)(2,1)}, u32[]{:S(2)}) copy-start(bf16[128,8,8,128]{3,2,1,0:T(8,128)(2,1)} %copy-done.1) | copy-start | bytes 6291460

commit v2 on v1

--- a/solution.py
+++ b/solution.py
@@ -14,11 +14,14 @@
 SLOTS = 16
 TAPS = 16
 HALO = 8
-PITCH = 32
+PITCH = 40
 GROUP = 8
-Q_CHUNKS = (4, 4, 4, 4)
+Q_CHUNKS = (4, 8, 4)
 POWER_CHUNK = 1
-INPUT_CHUNKS = 4
+IN_FLIGHT = 3
+SPECTRUM_BLOCK = 4
+CORRELATE_BLOCK = 1
+INPUT_CHUNKS = (16, 16, 16, 16)
 
 
 def real_dft(values):
@@ -101,10 +104,10 @@
     lax.fori_loop(0, frames, butterfly, 0)
 
 
-def filter_call(flag, voltages, before, after, taps, partial, chunk):
+def filter_call(flag, voltages, before, after, taps, partial, start):
     inputs, frames, length = voltages.shape
     groups = before.shape[0] // GROUP
-    base = chunk * groups
+    base = start // GROUP
     tiles = length // LANES
     operands = [flag, voltages, before, after, taps]
     in_specs = [
@@ -122,6 +125,9 @@
     return pl.pallas_call(
         filter_body,
         name="filter",
+        cost_estimate=pl.CostEstimate(
+            flops=groups * 5 * 10**9, transcendentals=0, bytes_accessed=groups * 4 * 2**20
+        ),
         grid=(groups,),
         in_specs=in_specs,
         out_specs=pl.BlockSpec((SLOTS, frames, GROUP, 2 * LANES), lambda g: (0, 0, g + base, 0)),
@@ -131,7 +137,7 @@
             pltpu.VMEM((frames, tiles, GROUP, LANES), jnp.float32),
         ],
         input_output_aliases=aliases,
-        compiler_params=pltpu.CompilerParams(vmem_limit_bytes=48 * 2**20),
+        compiler_params=pltpu.CompilerParams(vmem_limit_bytes=56 * 2**20),
     )(*operands)
 
 
@@ -150,84 +156,90 @@
     first, part_ref, cos_ref, sin_ref, twist_cos_ref, twist_sin_ref, gain_ref, out_ref, power_ref, turn_ref
 ):
     step = pl.program_id(0)
-    is_first = (step + first) == 0
-    rows = part_ref.shape[1] * part_ref.shape[2]
+    slots, frames, inputs, width = part_ref.shape
+    rows = frames * inputs
     odd = lax.broadcasted_iota(jnp.int32, (LANES, LANES), 0) % 2 == 1
-    twist_cos = jnp.where(odd, twist_cos_ref[0, 1:2, :], twist_cos_ref[0, 0:1, :])
-    twist_sin = jnp.where(odd, twist_sin_ref[0, 1:2, :], twist_sin_ref[0, 0:1, :])
-    cos = cos_ref[...] * twist_cos - sin_ref[...] * twist_sin
-    sin = sin_ref[...] * twist_cos + cos_ref[...] * twist_sin
-    special = jnp.where(is_first, 1.0, 0.0)
-    drop = jnp.where(odd, special, 0.0)
-    keep = 1.0 - drop
-    sign = jnp.where(odd, -1.0, 1.0) * (1.0 - special)
-    matrix = jnp.concatenate(
-        [
-            jnp.concatenate([cos * keep, sign * sin + drop * cos], axis=1),
-            jnp.concatenate([-sin * keep, sign * cos - drop * sin], axis=1),
-        ],
-        axis=0,
-    )
-    matrix_high, matrix_low = split(matrix)
-    part = part_ref[0].reshape(rows, 2 * LANES)
-    gain = gain_ref[0]
-    width = 2 * LANES
-    for block in range(rows // width):
-        part_high, part_low = split(part[block * width : (block + 1) * width])
-        spec = (
-            matmul_nt(matrix_high, part_high)
-            + matmul_nt(matrix_high, part_low)
-            + matmul_nt(matrix_low, part_high)
+    flip = jnp.where(odd, -1.0, 1.0)
+    per_block = width // LANES
+    total = None
+    for slot in range(slots):
+        twist_cos = jnp.where(odd, twist_cos_ref[slot, 1:2, :], twist_cos_ref[slot, 0:1, :])
+        twist_sin = jnp.where(odd, twist_sin_ref[slot, 1:2, :], twist_sin_ref[slot, 0:1, :])
+        cos = cos_ref[...] * twist_cos - sin_ref[...] * twist_sin
+        sin = sin_ref[...] * twist_cos + cos_ref[...] * twist_sin
+        parts = [cos, flip * sin, -sin, flip * cos]
+        if first == 0 and slot == 0:
+            special = jnp.where(step == 0, 1.0, 0.0)
+            drop = jnp.where(odd, special, 0.0)
+            keep = 1.0 - drop
+            sign = flip * (1.0 - special)
+            parts = [cos * keep, sign * sin + drop * cos, -sin * keep, sign * cos - drop * sin]
+        matrix = jnp.concatenate(
+            [jnp.concatenate(parts[:2], axis=1), jnp.concatenate(parts[2:], axis=1)], axis=0
         )
+        matrix_high, matrix_low = split(matrix)
+        part = part_ref[slot].reshape(rows, width)
+        gain = gain_ref[slot]
+        for block in range(rows // width):
+            part_high, part_low = split(part[block * width : (block + 1) * width])
+            spec = (
+                matmul_nt(matrix_high, part_high)
+                + matmul_nt(matrix_high, part_low)
+                + matmul_nt(matrix_low, part_high)
+            )
+            for side in range(2):
+                for tile in range(per_block):
+                    value = spec[
+                        side * LANES : (side + 1) * LANES, tile * LANES : (tile + 1) * LANES
+                    ]
+                    turn_ref[slot % 2, side, pl.ds(block * per_block + tile, LANES, stride=8), :] = (
+                        value * gain
+                    )
         for side in range(2):
-            for tile in range(width // LANES):
-                value = spec[side * LANES : (side + 1) * LANES, tile * LANES : (tile + 1) * LANES]
-                turn_ref[side, pl.ds(block * (width // LANES) + tile, LANES, stride=8), :] = (
-                    value * gain
-                )
-    power = jnp.zeros((8, LANES), jnp.float32)
-    for side in range(2):
-        rounded = turn_ref[side].reshape(LANES, 8, LANES).astype(jnp.bfloat16)
-        out_ref[:, side] = rounded
-        wide = rounded.astype(jnp.float32)
-        power = power + jnp.sum(wide * wide, axis=0)
+            rounded = turn_ref[slot % 2, side].reshape(LANES, 8, LANES).astype(jnp.bfloat16)
+            out_ref[:, 2 * slot + side] = rounded
+            wide = rounded.astype(jnp.float32)
+            power = jnp.sum(wide * wide, axis=0)
+            total = power if total is None else total + power
 
     @pl.when(step == 0)
     def _():
-        power_ref[...] = power
+        power_ref[...] = total
 
     @pl.when(step > 0)
     def _():
-        power_ref[...] += power
+        power_ref[...] += total
 
 
 def spectrum_call(partial, tables, gains, first, count, spare):
     _, frames, inputs, width = partial.shape
     cos, sin, twist_cos, twist_sin = tables
     whole = lambda q: (0, 0)
-    pick = lambda q: (q + first, 0, 0)
+    block = SPECTRUM_BLOCK
+    start = first // block
+    pick = lambda q: (q + start, 0, 0)
     return pl.pallas_call(
         functools.partial(spectrum_body, first),
         name="spectrum",
-        grid=(count,),
+        grid=(count // block,),
         in_specs=[
-            pl.BlockSpec((1, frames, inputs, width), lambda q: (q + first, 0, 0, 0)),
+            pl.BlockSpec((block, frames, inputs, width), lambda q: (q + start, 0, 0, 0)),
             pl.BlockSpec((LANES, LANES), whole),
             pl.BlockSpec((LANES, LANES), whole),
-            pl.BlockSpec((1, 2, LANES), pick),
-            pl.BlockSpec((1, 2, LANES), pick),
-            pl.BlockSpec((1, LANES, LANES), pick),
+            pl.BlockSpec((block, 2, LANES), pick),
+            pl.BlockSpec((block, 2, LANES), pick),
+            pl.BlockSpec((block, LANES, LANES), pick),
         ],
         out_specs=[
-            pl.BlockSpec((LANES, 2, 8, LANES), lambda q: (0, q, 0, 0)),
+            pl.BlockSpec((LANES, 2 * block, 8, LANES), lambda q: (0, q, 0, 0)),
             pl.BlockSpec((8, LANES), whole),
         ],
         out_shape=[
             jax.ShapeDtypeStruct((LANES, 2 * count + spare, 8, LANES), jnp.bfloat16),
             jax.ShapeDtypeStruct((8, LANES), jnp.float32),
         ],
-        scratch_shapes=[pltpu.VMEM((2, 8 * LANES, LANES), jnp.float32)],
-        compiler_params=pltpu.CompilerParams(vmem_limit_bytes=48 * 2**20),
+        scratch_shapes=[pltpu.VMEM((2, 2, 8 * LANES, LANES), jnp.float32)],
+        compiler_params=pltpu.CompilerParams(vmem_limit_bytes=56 * 2**20),
     )(partial, cos, sin, twist_cos, twist_sin, gains)
 
 
@@ -264,12 +276,13 @@
 
 def correlate_body(groups, odd_ref, spec_ref, row_ref, col_ref, *rest):
     out_ref, left_ref, swapped_ref = rest[-3:]
+    slot = pl.program_id(1)
     blocks = spec_ref.shape[0] // groups
     half = LANES // 2
     depth = blocks * 8
     for side in range(2):
         for s in range(groups):
-            tile = spec_ref[s * blocks : (s + 1) * blocks, side].reshape(depth, LANES).T
+            tile = spec_ref[s * blocks : (s + 1) * blocks, 2 * slot + side].reshape(depth, LANES).T
             rows = slice(s * half, (s + 1) * half)
             for part in range(2):
                 piece = tile[part * half : (part + 1) * half]
@@ -300,12 +313,17 @@
 
 def correlate_call(odd, spectra, scale_row, scale_col, visibilities, first, count, groups, channels):
     total = scale_row.shape[1]
-    place = lambda q, odd: (jnp.where(odd[0] == 1, (SLOTS - first - q) % SLOTS, first + q), 0, 0)
+    block = CORRELATE_BLOCK
+
+    def place(q, slot, odd):
+        at = first + q * block + slot
+        return (jnp.where(odd[0] == 1, (SLOTS - at) % SLOTS, at), 0, 0)
+
     operands = [odd, spectra, scale_row, scale_col]
     in_specs = [
-        pl.BlockSpec((spectra.shape[0], 2, 8, LANES), lambda q, odd: (0, q, 0, 0)),
-        pl.BlockSpec((1, total), lambda q, odd: (0, 0)),
-        pl.BlockSpec((total, 1), lambda q, odd: (0, 0)),
+        pl.BlockSpec((spectra.shape[0], 2 * block, 8, LANES), lambda q, slot, odd: (0, q, 0, 0)),
+        pl.BlockSpec((1, total), lambda q, slot, odd: (0, 0)),
+        pl.BlockSpec((total, 1), lambda q, slot, odd: (0, 0)),
     ]
     aliases = {}
     if visibilities is not None:
@@ -318,7 +336,7 @@
         name="correlate",
         grid_spec=pltpu.PrefetchScalarGridSpec(
             num_scalar_prefetch=1,
-            grid=(count,),
+            grid=(count // block, block),
             in_specs=in_specs,
             out_specs=pl.BlockSpec((1, total, total), place),
             scratch_shapes=[
@@ -328,7 +346,7 @@
         ),
         out_shape=jax.ShapeDtypeStruct((channels, total, total), jnp.float32),
         input_output_aliases=aliases,
-        compiler_params=pltpu.CompilerParams(vmem_limit_bytes=48 * 2**20),
+        compiler_params=pltpu.CompilerParams(vmem_limit_bytes=56 * 2**20),
     )(*operands)
 
 
@@ -342,14 +360,29 @@
     return [jnp.asarray(table, jnp.float32) for table in tables]
 
 
+def gains_body(gain_ref, out_ref, turned_ref):
+    inputs, channels = gain_ref.shape
+    half = LANES // 2
+    for block in range(channels // LANES):
+        piece = gain_ref[:, block * LANES : (block + 1) * LANES]
+        doubled = jnp.concatenate([piece] * (LANES // inputs), axis=0)
+        turned_ref[block * LANES : (block + 1) * LANES, :] = doubled.T
+    for q in range(SLOTS):
+        out_ref[q, pl.ds(0, half, stride=2), :] = turned_ref[pl.ds(q, half, stride=2 * SLOTS), :]
+        mirror = SLOTS + (SLOTS - q) % SLOTS
+        out_ref[q, pl.ds(1, half, stride=2), :] = turned_ref[
+            pl.ds(mirror, half, stride=2 * SLOTS), :
+        ]
+
+
 def arrange_gains(gains):
     inputs, channels = gains.shape
-    turned = gains.T.reshape(channels // (2 * SLOTS), 2, SLOTS, inputs)
-    straight = turned[:, 0]
-    reversed_ = jnp.roll(jnp.flip(turned[:, 1], axis=1), 1, axis=1)
-    both = jnp.stack([straight, reversed_], axis=1).reshape(channels // SLOTS, SLOTS, inputs)
-    by_slot = jnp.transpose(both, (1, 0, 2))
-    return jnp.concatenate([by_slot, by_slot], axis=2)
+    return pl.pallas_call(
+        gains_body,
+        name="gains",
+        out_shape=jax.ShapeDtypeStruct((SLOTS, channels // SLOTS, LANES), jnp.float32),
+        scratch_shapes=[pltpu.VMEM((channels, LANES), jnp.float32)],
+    )(gains)
 
 
 def per_device(voltages, pfb_taps, eq_gains):
@@ -360,22 +393,24 @@
     forward = [(i, i + 1) for i in range(times - 1)]
     backward = [((i + 1) % times, i) for i in range(times)]
     flag = jnp.where(here == times - 1, 0.0, 1.0).astype(jnp.float32).reshape(1)
-    size = inputs // INPUT_CHUNKS
-    halos = []
-    for chunk in range(INPUT_CHUNKS):
-        block = voltages[chunk * size : (chunk + 1) * size]
+    halos, start, source = [], 0, voltages
+    for index, size in enumerate(INPUT_CHUNKS):
+        block = source[start : start + size]
+        ends = (block[:, frames - HALO :], block[:, :HALO])
+        start += size
+        if index == 0:
+            source, *ends = lax.optimization_barrier((source, *ends))
+        if index >= IN_FLIGHT:
+            ends = lax.optimization_barrier((*ends, *halos[index - IN_FLIGHT]))[:2]
         halos.append(
-            (
-                lax.ppermute(block[:, frames - HALO :], "tm", forward),
-                lax.ppermute(block[:, :HALO], "tm", backward),
-            )
+            (lax.ppermute(ends[0], "tm", forward), lax.ppermute(ends[1], "tm", backward))
         )
     gains = arrange_gains(eq_gains)
     tables = trig_tables()
-    partial = None
-    for chunk in range(INPUT_CHUNKS):
-        before, after = halos[chunk]
-        partial = filter_call(flag, voltages, before, after, pfb_taps, partial, chunk)
+    partial, start = None, 0
+    for size, (before, after) in zip(INPUT_CHUNKS, halos):
+        partial = filter_call(flag, voltages, before, after, pfb_taps, partial, start)
+        start += size
     payloads, powers, first = [], [], 0
     for index, count in enumerate(Q_CHUNKS):
         spare = 1 if index == POWER_CHUNK else 0

time: 267 us -> 230 us (0.86)
  waiting for transfers between devices: 68.3 us -> 24.8 us
  blocking collectives: 37.7 us -> 61.8 us
  local copies, waits for them, and re-layouts: 25.2 us -> 12.4 us
  other arithmetic: 4.36 us -> 1.19 us
    all_to_all x3 -> x2, waiting for transfers between devices: 53.7 us -> 24.8 us  [per_device(): lax.all_to_all(payload, ('stn', 'tm'), split_axis=0, concat_axis=0, tiled...]
    all_to_all x1, blocking collectives: 37.7 us -> 61.8 us  [per_device(): lax.all_to_all(payload, ('stn', 'tm'), split_axis=0, concat_axis=0, tiled...]
    ppermute x8, waiting for transfers between devices: 14.6 us -> 0.02 us  [the longest x4 0.01 us: per_device(): lax.ppermute(ends[0], 'tm', forward)]
    unnamed x42 -> x8, local copies, waits for them, and re-layouts: 14.6 us -> 2.92 us
    pallas_call x4 -> x5, Pallas kernels: 51.2 us -> 47.5 us  [the longest x4 44.7 us: filter_call(): pl.pallas_call(filter_body, name='filter', cost_estimate=pl.CostEstimate(...]
    all_to_all x3 -> x2, starting transfers between devices: 22.9 us -> 19.9 us  [per_device(): lax.all_to_all(payload, ('stn', 'tm'), split_axis=0, concat_axis=0, tiled...]
    pallas_call x4 -> x3, Pallas kernels: 19.9 us -> 21.4 us  [correlate_call(): pl.pallas_call(functools.partial(correlate_body, groups), name='correlate...]
    pallas_call x4 -> x3, Pallas kernels: 21.3 us -> 22 us  [spectrum_call(): pl.pallas_call(functools.partial(spectrum_body, first), name='spectrum',...]
  transfers between devices with their start and end apart: 11 -> 10, of which waited for: 5 -> 2; matrix products, arithmetic and copies ran while one was open for 5% -> 3% of each run, Pallas kernels for 26% -> 30%
where the time goes in v2:
time: 230 us; the launch traced here: 229 us
  Pallas kernels  92.4 us (40%)
  blocking collectives  61.8 us (27%)
  starting transfers between devices  35.9 us (16%)
  waiting for transfers between devices  24.8 us (11%)
  local copies, waits for them, and re-layouts  12.4 us (5%)
    all_to_all x1, blocking collectives, per_device(): lax.all_to_all(payload, ('stn', 'tm'), split_axis=0, concat_axis=0, tiled...  61.8 us
    pallas_call x4, Pallas kernels, filter_call(): pl.pallas_call(filter_body, name='filter', cost_estimate=pl.CostEstimate(...  44.7 us
    all_to_all x2, waiting for transfers between devices, per_device(): lax.all_to_all(payload, ('stn', 'tm'), split_axis=0, concat_axis=0, tiled...  24.8 us
    pallas_call x3, Pallas kernels, spectrum_call(): pl.pallas_call(functools.partial(spectrum_body, first), name='spectrum',...  22 us
    pallas_call x3, Pallas kernels, correlate_call(): pl.pallas_call(functools.partial(correlate_body, groups), name='correlate...  21.4 us
    all_to_all x2, starting transfers between devices, per_device(): lax.all_to_all(payload, ('stn', 'tm'), split_axis=0, concat_axis=0, tiled...  19.9 us
    ppermute x4, starting transfers between devices, per_device(): lax.ppermute(ends[0], 'tm', forward)  14.3 us
    slice x2, local copies, waits for them, and re-layouts, per_device(): ends = (block[:, frames - HALO:], block[:, :HALO])  7.79 us
  transfers between devices with their start and end apart: 10, of which 2 were waited for; matrix products, arithmetic and copies ran while one was open for 3% of the time, Pallas kernels for 30%

profile of v2, /device:TPU:1, one launch (start us, length us, event | category | flops | bytes accessed | tf_op | source)
XLA Modules:
  0.0 228.6 jit_solution(12084610732928641058)
XLA Ops:
  0.0 3.1 %fusion.1 = (bf16[16,8,4096]{2,1,0:T(8,128)(2,1)}, bf16[16,8,4096]{2,1,0:T(8,128)(2,1)}) fusion(bf16[64,16,4096]{2,1,0:T(8,128)(2,1)} %own_ref.7), kind=kLoop, calls=%fused_computation.4 | loop fusion | bytes 4194304 | tf_op jit(solution)/shard_map/slice | solution.py:399
  3.1 4.9 %collective-permute-start = (bf16[16,8,4096]{2,1,0:T(8,128)(2,1)}, bf16[16,8,4096]{2,1,0:T(8,128)(2,1)}, u32[]{:S(2)}, u32[]{:S(2)}) collective-permute-start(bf16[16,8,4096]{2,1,0:T(8,128)(2,1)} %get-tuple-element.17), channel_id=1, source_target_pairs={{0,1},{1,2},{2,3},{3,4},{4,5},{5,6},{6,7},{7,8},{8,9},{9,10},{10,1... | collective-permute-start | bytes 3145736 | tf_op jit(solution)/shard_map/ppermute | solution.py:406
  8.1 4.7 %fusion = (bf16[16,8,4096]{2,1,0:T(8,128)(2,1)}, bf16[16,8,4096]{2,1,0:T(8,128)(2,1)}, bf16[16,8,4096]{2,1,0:T(8,128)(2,1)S(1)}, bf16[16,8,4096]{2,1,0:T(8,128)(...) fusion(bf16[64,16,4096]{2,1,0:T(8,128)(2,1)} %own_ref.7), kind=kLoop, calls=%fused_computation.3 | loop fusion | bytes 12582912 | tf_op jit(solution)/shard_map/slice | solution.py:399
  12.8 3.6 %collective-permute-start.6 = (bf16[16,8,4096]{2,1,0:T(8,128)(2,1)}, bf16[16,8,4096]{2,1,0:T(8,128)(2,1)}, u32[]{:S(2)}, u32[]{:S(2)}) collective-permute-start(bf16[16,8,4096]{2,1,0:T(8,128)(2,1)} %get-tuple-element.28), channel_id=1, source_target_pairs={{0,1},{1,2},{2,3},{3,4},{4,5},{5,6},{6,7},{7,8},{8,9},{9,10},{10,1... | collective-permute-start | bytes 3145736 | tf_op jit(solution)/shard_map/ppermute | solution.py:406
  16.4 1.0 collective-permute-start.7
  17.4 2.8 %collective-permute-start.4 = (bf16[16,8,4096]{2,1,0:T(8,128)(2,1)}, bf16[16,8,4096]{2,1,0:T(8,128)(2,1)}, u32[]{:S(2)}, u32[]{:S(2)}) collective-permute-start(bf16[16,8,4096]{2,1,0:T(8,128)(2,1)} %get-tuple-element.30), channel_id=1, source_target_pairs={{0,1},{1,2},{2,3},{3,4},{4,5},{5,6},{6,7},{7,8},{8,9},{9,10},{10,1... | collective-permute-start | bytes 3145736 | tf_op jit(solution)/shard_map/ppermute | solution.py:406
  20.2 2.8 %gains.1.gain_ref = f32[16,128,128]{2,1,0:T(8,128)} custom-call(f32[64,2048]{1,0:T(8,128)} %gain_ref.1), custom_call_target="tpu_custom_call" | custom-call | tf_op jit(solution)/shard_map/gains/pallas_call | solution.py:380
  22.9 0.6 collective-permute-start.5
  23.6 3.0 %collective-permute-start.2 = (bf16[16,8,4096]{2,1,0:T(8,128)(2,1)S(1)}, bf16[16,8,4096]{2,1,0:T(8,128)(2,1)S(1)}, u32[]{:S(2)}, u32[]{:S(2)}) collective-permute-start(bf16[16,8,4096]{2,1,0:T(8,128)(2,1)S(1)} %get-tuple-element.19), channel_id=1, source_target_pairs={{0,1},{1,2},{2,3},{3,4},{4,5},{5,6},{6,7},{7,8},{8,9},{9,10},{10,1... | collective-permute-start | bytes 3145736 | tf_op jit(solution)/shard_map/ppermute | solution.py:406
  26.6 11.2 %filter.4.rest_0_ = f32[16,16,64,256]{3,2,1,0:T(8,128)} custom-call(f32[1]{0:T(128)} %bitcast.1.flag_ref, bf16[64,16,4096]{2,1,0:T(8,128)(2,1)} %own_ref.7, bf16[16,8,4096]{2,1,0:T(8,128)(2,1)} %collective-permute-done.before_ref, bf16[16,8,4096]{2,1,0:T(8,128)(2,1)} %collective-permute-done.1.after_ref, f32[16,4096]{1,0:T(8,128)} %taps_ref.7), custom_call_target="tpu_custom_call" | custom-call | flops 10000000000 | bytes 8388608 | tf_op jit(solution)/shard_map/filter/pallas_call | solution.py:125
  37.8 11.2 %filter.5.rest_0_ = f32[16,16,64,256]{3,2,1,0:T(8,128)} custom-call(f32[1]{0:T(128)} %bitcast.1.flag_ref, bf16[64,16,4096]{2,1,0:T(8,128)(2,1)} %own_ref.7, bf16[16,8,4096]{2,1,0:T(8,128)(2,1)} %collective-permute-done.6.before_ref, bf16[16,8,4096]{2,1,0:T(8,128)(2,1)} %collective-permute-done.7.after_ref, ...), custom_call_target="tpu_custom_call", output_to_operand_aliasing={{}: (5, {})} | custom-call | flops 10000000000 | bytes 8388608 | tf_op jit(solution)/shard_map/filter/pallas_call | solution.py:125
  49.0 1.0 copy-done.2
  50.0 11.2 %filter.6.rest_0_ = f32[16,16,64,256]{3,2,1,0:T(8,128)} custom-call(f32[1]{0:T(128)} %bitcast.1.flag_ref, bf16[64,16,4096]{2,1,0:T(8,128)(2,1)} %own_ref.7, bf16[16,8,4096]{2,1,0:T(8,128)(2,1)} %collective-permute-done.4.before_ref, bf16[16,8,4096]{2,1,0:T(8,128)(2,1)} %copy-done.2, f32[16,4096]{1,0:T(8,128)} %taps_ref.7, ...), custom_call_target="tpu_custom_call", output_to_operand_aliasing={{}: (5, {})} | custom-call | flops 10000000000 | bytes 8388608 | tf_op jit(solution)/shard_map/filter/pallas_call | solution.py:125
  61.2 1.0 copy-done.1
  62.2 1.0 copy-done.3
  63.1 11.2 %filter.7.part_ref = f32[16,16,64,256]{3,2,1,0:T(8,128)} custom-call(f32[1]{0:T(128)} %bitcast.1.flag_ref, bf16[64,16,4096]{2,1,0:T(8,128)(2,1)} %own_ref.7, bf16[16,8,4096]{2,1,0:T(8,128)(2,1)} %copy-done.1, bf16[16,8,4096]{2,1,0:T(8,128)(2,1)} %copy-done.3, f32[16,4096]{1,0:T(8,128)} %taps_ref.7, ...), custom_call_target="tpu_custom_call", output_to_operand_aliasing={{}: (5, {})} | custom-call | flops 10000000000 | bytes 8388608 | tf_op jit(solution)/shard_map/filter/pallas_call | solution.py:125
  74.3 6.4 %spectrum.4 = (bf16[128,8,8,128]{3,2,1,0:T(8,128)(2,1)}, f32[8,128]{1,0:T(8,128)}) custom-call(f32[16,16,64,256]{3,2,1,0:T(8,128)} %filter.7.part_ref, f32[128,128]{1,0:T(8,128)} %constant.39.clone.cos_ref, f32[128,128]{1,0:T(8,128)} %constant.40.clone.sin_ref, f32[16,2,128]{2,1,0:T(2,128)} %constant.41.clone.twist_cos_ref, ...), custom_call_target="tpu_custom_call" | custom-call | tf_op jit(solution)/shard_map/spectrum/pallas_call | solution.py:221
  80.7 14.9 %all-to-all-start.2 = ((bf16[128,8,8,128]{3,2,1,0:T(8,128)(2,1)}), bf16[128,8,8,128]{3,2,1,0:T(8,128)(2,1)S(1)}, u32[]{:S(2)}, u32[]{:S(2)}) async-start(bf16[128,8,8,128]{3,2,1,0:T(8,128)(2,1)} %get-tuple-element.26), calls=%async_computation.2 | async-start | bytes 4194304 | tf_op jit(solution)/shard_map/all_to_all | solution.py:423
  95.6 6.3 %spectrum.3 = (bf16[128,8,8,128]{3,2,1,0:T(8,128)(2,1)}, f32[8,128]{1,0:T(8,128)}) custom-call(f32[16,16,64,256]{3,2,1,0:T(8,128)} %filter.7.part_ref, f32[128,128]{1,0:T(8,128)} %constant.39.clone.cos_ref, f32[128,128]{1,0:T(8,128)} %constant.40.clone.sin_ref, f32[16,2,128]{2,1,0:T(2,128)} %constant.41.clone.twist_cos_ref, ...), custom_call_target="tpu_custom_call" | custom-call | tf_op jit(solution)/shard_map/spectrum/pallas_call | solution.py:221
  101.9 9.3 %spectrum.5 = (bf16[128,17,8,128]{3,2,1,0:T(8,128)(2,1)}, f32[8,128]{1,0:T(8,128)}) custom-call(f32[16,16,64,256]{3,2,1,0:T(8,128)} %filter.7.part_ref, f32[128,128]{1,0:T(8,128)} %constant.39.clone.cos_ref, f32[128,128]{1,0:T(8,128)} %constant.40.clone.sin_ref, f32[16,2,128]{2,1,0:T(2,128)} %constant.41.clone.twist_cos_ref, ...), custom_call_target="tpu_custom_call" | custom-call | tf_op jit(solution)/shard_map/spectrum/pallas_call | solution.py:221
  111.2 1.5 stamp.1
  112.7 13.3 %all-to-all-done.2.spec_ref = bf16[128,8,8,128]{3,2,1,0:T(8,128)(2,1)S(1)} async-done(((bf16[128,8,8,128]{3,2,1,0:T(8,128)(2,1)}), bf16[128,8,8,128]{3,2,1,0:T(8,128)(2,1)S(1)}, u32[]{:S(2)}, u32[]{:S(2)}) %all-to-all-start.2) | async-done | bytes 2097184 | tf_op jit(solution)/shard_map/all_to_all | solution.py:423
  126.0 61.8 %all_to_all.15.spec_ref = bf16[128,17,8,128]{3,2,1,0:T(8,128)(2,1)} all-to-all(bf16[128,17,8,128]{3,2,1,0:T(8,128)(2,1)} %stamp.1), channel_id=1, replica_groups=mesh['stn'=8,'tm'=16] {'stn','tm'}, dimensions={0} | all-to-all | bytes 8912896 | tf_op jit(solution)/shard_map/all_to_all | solution.py:423
  187.8 5.0 %all-to-all-start = ((bf16[128,8,8,128]{3,2,1,0:T(8,128)(2,1)}), bf16[128,8,8,128]{3,2,1,0:T(8,128)(2,1)}, u32[]{:S(2)}, u32[]{:S(2)}) async-start(bf16[128,8,8,128]{3,2,1,0:T(8,128)(2,1)} %get-tuple-element.21), calls=%async_computation | async-start | bytes 4194304 | tf_op jit(solution)/shard_map/all_to_all | solution.py:423
  192.9 1.1 convert_reduce_fusion
  194.0 0.1 reduce_sum.14
  194.2 0.7 div.18.row_ref
  194.9 0.9 rsqrt.23.col_ref
  195.8 5.7 %correlate.3.rest_0_ = f32[16,512,512]{2,1,0:T(8,128)} custom-call(s32[1]{0:T(128)} %bitcast.odd_ref, bf16[128,8,8,128]{3,2,1,0:T(8,128)(2,1)} %copy-done, f32[1,512]{1,0:T(1,128)} %div.18.row_ref, f32[512,1]{1,0:T(8,128)} %rsqrt.23.col_ref), custom_call_target="tpu_custom_call" | custom-call | tf_op jit(solution)/shard_map/correlate/pallas_call | solution.py:334
  201.5 10.0 %correlate.4.rest_0_ = f32[16,512,512]{2,1,0:T(8,128)} custom-call(s32[1]{0:T(128)} %bitcast.odd_ref, bf16[128,17,8,128]{3,2,1,0:T(8,128)(2,1)} %all_to_all.15.spec_ref, f32[1,512]{1,0:T(1,128)} %div.18.row_ref, f32[512,1]{1,0:T(8,128)} %rsqrt.23.col_ref, f32[16,512,512]{2,1,0:T(8,128)} %correlate.3.rest_0_), custom_call_target="tpu_custom_call", output_to_operand_aliasing={{}: (4, {})} | custom-call | tf_op jit(solution)/shard_map/correlate/pallas_call | solution.py:334
  211.5 11.4 %all-to-all-done.spec_ref = bf16[128,8,8,128]{3,2,1,0:T(8,128)(2,1)} async-done(((bf16[128,8,8,128]{3,2,1,0:T(8,128)(2,1)}), bf16[128,8,8,128]{3,2,1,0:T(8,128)(2,1)}, u32[]{:S(2)}, u32[]{:S(2)}) %all-to-all-start) | async-done | bytes 2097184 | tf_op jit(solution)/shard_map/all_to_all | solution.py:423
  222.9 5.7 %correlate.5 = f32[16,512,512]{2,1,0:T(8,128)} custom-call(s32[1]{0:T(128)} %bitcast.odd_ref, bf16[128,8,8,128]{3,2,1,0:T(8,128)(2,1)} %all-to-all-done.spec_ref, f32[1,512]{1,0:T(1,128)} %div.18.row_ref, f32[512,1]{1,0:T(8,128)} %rsqrt.23.col_ref, f32[16,512,512]{2,1,0:T(8,128)} %correlate.4.rest_0_), custom_call_target="tpu_custom_call", output_to_operand_aliasing={{}: (4, {})} | custom-call | tf_op jit(solution)/shard_map/correlate/pallas_call | solution.py:334
  (17 shorter events, 0.2 us)
Async XLA Ops:
  3.1 19.8 %collective-permute-start = (bf16[16,8,4096]{2,1,0:T(8,128)(2,1)}, bf16[16,8,4096]{2,1,0:T(8,128)(2,1)}, u32[]{:S(2)}, u32[]{:S(2)}) collective-permute-start(bf16[16,8,4096]{2,1,0:T(8,128)(2,1)} %get-tuple-element.17), channel_id=1, source_target_pairs={{0,1},{1,2},{2,3},{3,4},{4,5},{5,6},{6,7},{7,8},{8,9},{9,10},{10,1... | collective-permute-start | bytes 3145736 | tf_op jit(solution)/shard_map/ppermute | solution.py:406
  8.0 15.5 %collective-permute-start.1 = (bf16[16,8,4096]{2,1,0:T(8,128)(2,1)}, bf16[16,8,4096]{2,1,0:T(8,128)(2,1)}, u32[]{:S(2)}, u32[]{:S(2)}) collective-permute-start(bf16[16,8,4096]{2,1,0:T(8,128)(2,1)} %get-tuple-element.18), channel_id=1, source_target_pairs={{1,0},{2,1},{3,2},{4,3},{5,4},{6,5},{7,6},{8,7},{9,8},{10,9},{11,1... | collective-permute-start | bytes 3145736 | tf_op jit(solution)/shard_map/ppermute | solution.py:406
  12.8 25.0 %collective-permute-start.6 = (bf16[16,8,4096]{2,1,0:T(8,128)(2,1)}, bf16[16,8,4096]{2,1,0:T(8,128)(2,1)}, u32[]{:S(2)}, u32[]{:S(2)}) collective-permute-start(bf16[16,8,4096]{2,1,0:T(8,128)(2,1)} %get-tuple-element.28), channel_id=1, source_target_pairs={{0,1},{1,2},{2,3},{3,4},{4,5},{5,6},{6,7},{7,8},{8,9},{9,10},{10,1... | collective-permute-start | bytes 3145736 | tf_op jit(solution)/shard_map/ppermute | solution.py:406
  16.4 21.4 %collective-permute-start.7 = (bf16[16,8,4096]{2,1,0:T(8,128)(2,1)}, bf16[16,8,4096]{2,1,0:T(8,128)(2,1)}, u32[]{:S(2)}, u32[]{:S(2)}) collective-permute-start(bf16[16,8,4096]{2,1,0:T(8,128)(2,1)} %get-tuple-element.27), channel_id=1, source_target_pairs={{1,0},{2,1},{3,2},{4,3},{5,4},{6,5},{7,6},{8,7},{9,8},{10,9},{11,1... | collective-permute-start | bytes 3145736 | tf_op jit(solution)/shard_map/ppermute | solution.py:406
  17.4 31.6 %collective-permute-start.4 = (bf16[16,8,4096]{2,1,0:T(8,128)(2,1)}, bf16[16,8,4096]{2,1,0:T(8,128)(2,1)}, u32[]{:S(2)}, u32[]{:S(2)}) collective-permute-start(bf16[16,8,4096]{2,1,0:T(8,128)(2,1)} %get-tuple-element.30), channel_id=1, source_target_pairs={{0,1},{1,2},{2,3},{3,4},{4,5},{5,6},{6,7},{7,8},{8,9},{9,10},{10,1... | collective-permute-start | bytes 3145736 | tf_op jit(solution)/shard_map/ppermute | solution.py:406
  22.9 26.1 %collective-permute-start.5 = (bf16[16,8,4096]{2,1,0:T(8,128)(2,1)S(1)}, bf16[16,8,4096]{2,1,0:T(8,128)(2,1)S(1)}, u32[]{:S(2)}, u32[]{:S(2)}) collective-permute-start(bf16[16,8,4096]{2,1,0:T(8,128)(2,1)S(1)} %get-tuple-element.29), channel_id=1, source_target_pairs={{1,0},{2,1},{3,2},{4,3},{5,4},{6,5},{7,6},{8,7},{9,8},{10,9},{11,1... | collective-permute-start | bytes 3145736 | tf_op jit(solution)/shard_map/ppermute | solution.py:406
  23.6 37.6 %collective-permute-start.2 = (bf16[16,8,4096]{2,1,0:T(8,128)(2,1)S(1)}, bf16[16,8,4096]{2,1,0:T(8,128)(2,1)S(1)}, u32[]{:S(2)}, u32[]{:S(2)}) collective-permute-start(bf16[16,8,4096]{2,1,0:T(8,128)(2,1)S(1)} %get-tuple-element.19), channel_id=1, source_target_pairs={{0,1},{1,2},{2,3},{3,4},{4,5},{5,6},{6,7},{7,8},{8,9},{9,10},{10,1... | collective-permute-start | bytes 3145736 | tf_op jit(solution)/shard_map/ppermute | solution.py:406
  37.8 23.4 %collective-permute-start.3 = (bf16[16,8,4096]{2,1,0:T(8,128)(2,1)S(1)}, bf16[16,8,4096]{2,1,0:T(8,128)(2,1)S(1)}, u32[]{:S(2)}, u32[]{:S(2)}) collective-permute-start(bf16[16,8,4096]{2,1,0:T(8,128)(2,1)S(1)} %get-tuple-element.20), channel_id=1, source_target_pairs={{1,0},{2,1},{3,2},{4,3},{5,4},{6,5},{7,6},{8,7},{9,8},{10,9},{11,1... | collective-permute-start | bytes 3145736 | tf_op jit(solution)/shard_map/ppermute | solution.py:406
  49.0 1.0 copy-start.2
  61.2 1.0 copy-start.1
  62.2 1.0 copy-start.3
  80.7 45.3 %all-to-all-start.2 = ((bf16[128,8,8,128]{3,2,1,0:T(8,128)(2,1)}), bf16[128,8,8,128]{3,2,1,0:T(8,128)(2,1)S(1)}, u32[]{:S(2)}, u32[]{:S(2)}) async-start(bf16[128,8,8,128]{3,2,1,0:T(8,128)(2,1)} %get-tuple-element.26), calls=%async_computation.2 | async-start | bytes 4194304 | tf_op jit(solution)/shard_map/all_to_all | solution.py:423
  126.0 69.8 %copy-start = (bf16[128,8,8,128]{3,2,1,0:T(8,128)(2,1)}, bf16[128,8,8,128]{3,2,1,0:T(8,128)(2,1)S(1)}, u32[]{:S(2)}) copy-start(bf16[128,8,8,128]{3,2,1,0:T(8,128)(2,1)S(1)} %all-to-all-done.2.spec_ref) | copy-start | bytes 6291460
  187.8 35.1 %all-to-all-start = ((bf16[128,8,8,128]{3,2,1,0:T(8,128)(2,1)}), bf16[128,8,8,128]{3,2,1,0:T(8,128)(2,1)}, u32[]{:S(2)}, u32[]{:S(2)}) async-start(bf16[128,8,8,128]{3,2,1,0:T(8,128)(2,1)} %get-tuple-element.21), calls=%async_computation | async-start | bytes 4194304 | tf_op jit(solution)/shard_map/all_to_all | solution.py:423

commit v3 on v2

--- a/solution.py
+++ b/solution.py
@@ -16,12 +16,11 @@
 HALO = 8
 PITCH = 40
 GROUP = 8
-Q_CHUNKS = (4, 8, 4)
-POWER_CHUNK = 1
+Q_CHUNKS = (13, 3)
 IN_FLIGHT = 3
 SPECTRUM_BLOCK = 4
 CORRELATE_BLOCK = 1
-INPUT_CHUNKS = (16, 16, 16, 16)
+INPUT_CHUNKS = (24, 24, 16)
 
 
 def real_dft(values):
@@ -75,19 +74,36 @@
         taps = [
             jnp.broadcast_to(taps_ref[p : p + 1, lanes], (GROUP, LANES)) for p in range(TAPS)
         ]
+        even_taps, odd_taps = taps[0::2], taps[1::2]
+        both_taps = [a + b for a, b in zip(even_taps, odd_taps)]
+        depth = TAPS // 2
+
+        def frame(row, half):
+            value = frames_ref[pl.ds(tile * span + row, GROUP, stride=PITCH), :]
+            return value * flag if half == 1 and row < HALO + frames else value
+
+        def add(sums, at, term):
+            sums[at] = sums[at] + term if at in sums else term
+
         for half in range(2):
-            sums = [None] * HALO
-            for r in range(1 + 8 * half, 24 + 8 * half):
-                frame = frames_ref[pl.ds(tile * span + r, GROUP, stride=PITCH), :]
-                if half == 1 and r < HALO + frames:
-                    frame = frame * flag
-                for j in range(HALO):
-                    p = j + 8 * half + TAPS - r
-                    if 0 <= p < TAPS:
-                        term = taps[p] * frame
-                        sums[j] = term if sums[j] is None else sums[j] + term
-            for j in range(HALO):
-                filtered_ref[j + 8 * half, tile] = sums[j]
+            base = 4 * half
+            evens, odds, boths = {}, {}, {}
+            for s in range(base, base + 12):
+                odd = frame(2 * s + 1, half)
+                for i in range(base - 1, base + 4):
+                    if 0 <= i + depth - s < depth:
+                        add(odds, i, odd_taps[i + depth - s] * odd)
+                if s == base:
+                    continue
+                even = frame(2 * s, half)
+                both = even + odd
+                for i in range(base, base + 4):
+                    if 0 <= i + depth - s < depth:
+                        add(evens, i, even_taps[i + depth - s] * even)
+                        add(boths, i, both_taps[i + depth - s] * both)
+            for i in range(base, base + 4):
+                filtered_ref[2 * i, tile] = evens[i] + odds[i - 1]
+                filtered_ref[2 * i + 1, tile] = boths[i] - evens[i] - odds[i]
         return carry
 
     lax.fori_loop(0, tiles, fir, 0)
@@ -153,7 +169,16 @@
 
 
 def spectrum_body(
-    first, part_ref, cos_ref, sin_ref, twist_cos_ref, twist_sin_ref, gain_ref, out_ref, power_ref, turn_ref
+    part_ref,
+    cos_ref,
+    sin_ref,
+    twist_cos_ref,
+    twist_sin_ref,
+    gain_ref,
+    early_ref,
+    late_ref,
+    power_ref,
+    turn_ref,
 ):
     step = pl.program_id(0)
     slots, frames, inputs, width = part_ref.shape
@@ -168,7 +193,7 @@
         cos = cos_ref[...] * twist_cos - sin_ref[...] * twist_sin
         sin = sin_ref[...] * twist_cos + cos_ref[...] * twist_sin
         parts = [cos, flip * sin, -sin, flip * cos]
-        if first == 0 and slot == 0:
+        if slot == 0:
             special = jnp.where(step == 0, 1.0, 0.0)
             drop = jnp.where(odd, special, 0.0)
             keep = 1.0 - drop
@@ -197,7 +222,9 @@
                     )
         for side in range(2):
             rounded = turn_ref[slot % 2, side].reshape(LANES, 8, LANES).astype(jnp.bfloat16)
-            out_ref[:, 2 * slot + side] = rounded
+            early_ref[:, 2 * slot + side] = rounded
+            if slot >= slots - Q_CHUNKS[1]:
+                late_ref[:, 2 * (slot - slots + Q_CHUNKS[1]) + side] = rounded
             wide = rounded.astype(jnp.float32)
             power = jnp.sum(wide * wide, axis=0)
             total = power if total is None else total + power
@@ -210,20 +237,31 @@
     def _():
         power_ref[...] += total
 
-
-def spectrum_call(partial, tables, gains, first, count, spare):
+    @pl.when(step == pl.num_programs(0) - 1)
+    def _():
+        power = jnp.sum(power_ref[...], axis=0, keepdims=True)
+        high = power.astype(jnp.bfloat16).astype(jnp.float32)
+        middle = (power - high).astype(jnp.bfloat16).astype(jnp.float32)
+        low = power - high - middle
+        row = lax.broadcasted_iota(jnp.int32, (8, LANES), 0)
+        tile = jnp.where(row == 0, high, jnp.where(row == 1, middle, jnp.where(row == 2, low, 0.0)))
+        early_ref[:, 2 * (slots - Q_CHUNKS[1])] = jnp.broadcast_to(
+            tile.astype(jnp.bfloat16)[None], (LANES, 8, LANES)
+        )
+
+
+def spectrum_call(partial, tables, gains):
     _, frames, inputs, width = partial.shape
-    cos, sin, twist_cos, twist_sin = tables
+    block = SPECTRUM_BLOCK
     whole = lambda q: (0, 0)
-    block = SPECTRUM_BLOCK
-    start = first // block
-    pick = lambda q: (q + start, 0, 0)
+    pick = lambda q: (q, 0, 0)
+    early, late = Q_CHUNKS
     return pl.pallas_call(
-        functools.partial(spectrum_body, first),
+        spectrum_body,
         name="spectrum",
-        grid=(count // block,),
+        grid=(SLOTS // block,),
         in_specs=[
-            pl.BlockSpec((block, frames, inputs, width), lambda q: (q + start, 0, 0, 0)),
+            pl.BlockSpec((block, frames, inputs, width), lambda q: (q, 0, 0, 0)),
             pl.BlockSpec((LANES, LANES), whole),
             pl.BlockSpec((LANES, LANES), whole),
             pl.BlockSpec((block, 2, LANES), pick),
@@ -232,46 +270,18 @@
         ],
         out_specs=[
             pl.BlockSpec((LANES, 2 * block, 8, LANES), lambda q: (0, q, 0, 0)),
-            pl.BlockSpec((8, LANES), whole),
+            pl.BlockSpec((LANES, 2 * late, 8, LANES), lambda q: (0, 0, 0, 0)),
         ],
         out_shape=[
-            jax.ShapeDtypeStruct((LANES, 2 * count + spare, 8, LANES), jnp.bfloat16),
-            jax.ShapeDtypeStruct((8, LANES), jnp.float32),
+            jax.ShapeDtypeStruct((LANES, 2 * early + 1, 8, LANES), jnp.bfloat16),
+            jax.ShapeDtypeStruct((LANES, 2 * late, 8, LANES), jnp.bfloat16),
         ],
-        scratch_shapes=[pltpu.VMEM((2, 2, 8 * LANES, LANES), jnp.float32)],
+        scratch_shapes=[
+            pltpu.VMEM((8, LANES), jnp.float32),
+            pltpu.VMEM((2, 2, 8 * LANES, LANES), jnp.float32),
+        ],
         compiler_params=pltpu.CompilerParams(vmem_limit_bytes=56 * 2**20),
-    )(partial, cos, sin, twist_cos, twist_sin, gains)
-
-
-def stamp_body(*refs):
-    out_ref = refs[-1]
-    total = refs[0][...]
-    for ref in refs[1:-2]:
-        total = total + ref[...]
-    total = jnp.sum(total, axis=0, keepdims=True)
-    high, rest = total.astype(jnp.bfloat16), total
-    rest = rest - high.astype(jnp.float32)
-    middle = rest.astype(jnp.bfloat16)
-    low = (rest - middle.astype(jnp.float32)).astype(jnp.bfloat16)
-    row = lax.broadcasted_iota(jnp.int32, (8, LANES), 0)
-    tile = jnp.where(row == 0, high.astype(jnp.float32), 0.0)
-    tile = jnp.where(row == 1, middle.astype(jnp.float32), tile)
-    tile = jnp.where(row == 2, low.astype(jnp.float32), tile).astype(jnp.bfloat16)
-    out_ref[...] = jnp.broadcast_to(tile[None, None], out_ref.shape)
-
-
-def stamp_call(powers, payload):
-    last = payload.shape[1] - 1
-    return pl.pallas_call(
-        stamp_body,
-        name="stamp",
-        grid=(1,),
-        in_specs=[pl.BlockSpec((8, LANES), lambda i: (0, 0))] * len(powers)
-        + [pl.BlockSpec(memory_space=pl.ANY)],
-        out_specs=pl.BlockSpec((LANES, 1, 8, LANES), lambda i: (0, last, 0, 0)),
-        out_shape=jax.ShapeDtypeStruct(payload.shape, payload.dtype),
-        input_output_aliases={len(powers): 0},
-    )(*powers, payload)
+    )(partial, *tables, gains)
 
 
 def correlate_body(groups, odd_ref, spec_ref, row_ref, col_ref, *rest):
@@ -411,19 +421,12 @@
     for size, (before, after) in zip(INPUT_CHUNKS, halos):
         partial = filter_call(flag, voltages, before, after, pfb_taps, partial, start)
         start += size
-    payloads, powers, first = [], [], 0
-    for index, count in enumerate(Q_CHUNKS):
-        spare = 1 if index == POWER_CHUNK else 0
-        payload, power = spectrum_call(partial, tables, gains, first, count, spare)
-        payloads.append(payload)
-        powers.append(power)
-        first += count
-    payloads[POWER_CHUNK] = stamp_call(powers, payloads[POWER_CHUNK])
+    payloads = spectrum_call(partial, tables, gains)
     received = [
         lax.all_to_all(payload, ("stn", "tm"), split_axis=0, concat_axis=0, tiled=True)
         for payload in payloads
     ]
-    parts = received[POWER_CHUNK][:, 2 * Q_CHUNKS[POWER_CHUNK], :3].astype(jnp.float32)
+    parts = received[0][:, 2 * Q_CHUNKS[0], :3].astype(jnp.float32)
     parts = parts.reshape(stations, times, 3, LANES // inputs, inputs)
     power = jnp.sum(parts, axis=(1, 2, 3)).reshape(stations * inputs)
     all_frames = frames * times

time: 230 us -> 219 us (0.952)
  blocking collectives: 61.8 us -> 93.7 us
  starting transfers between devices: 35.9 us -> 18.7 us
  Pallas kernels: 92.4 us -> 79.1 us
  waiting for transfers between devices: 24.8 us -> 11.9 us
    all_to_all x1, blocking collectives: 61.8 us -> 93.7 us  [per_device(): lax.all_to_all(payload, ('stn', 'tm'), split_axis=0, concat_axis=0, tiled...]
    all_to_all x2 -> x1, waiting for transfers between devices: 24.8 us -> 6.32 us  [per_device(): lax.all_to_all(payload, ('stn', 'tm'), split_axis=0, concat_axis=0, tiled...]
    all_to_all x2 -> x1, starting transfers between devices: 19.9 us -> 6.35 us  [per_device(): lax.all_to_all(payload, ('stn', 'tm'), split_axis=0, concat_axis=0, tiled...]
    pallas_call x4 -> x1, Pallas kernels: 23.4 us -> 15.6 us  [spectrum_call(): pl.pallas_call(spectrum_body, name='spectrum', grid=(SLOTS // block,), in...]
    pallas_call x4 -> x3, Pallas kernels: 44.7 us -> 40.1 us  [filter_call(): pl.pallas_call(filter_body, name='filter', cost_estimate=pl.CostEstimate(...]
    ppermute x4 -> x3, waiting for transfers between devices: 0.01 us -> 4.55 us  [per_device(): lax.ppermute(ends[1], 'tm', backward)]
    ppermute x4 -> x3, starting transfers between devices: 14.3 us -> 11.2 us  [per_device(): lax.ppermute(ends[0], 'tm', forward)]
    slice x2 -> x3, local copies, waits for them, and re-layouts: 7.79 us -> 9.75 us  [per_device(): ends = (block[:, frames - HALO:], block[:, :HALO])]
  transfers between devices with their start and end apart: 10 -> 7, of which waited for: 2 -> 4; matrix products, arithmetic and copies ran while one was open for 3% -> 4% of each run, Pallas kernels for 30% -> 22%
where the time goes in v3:
time: 219 us; the launch traced here: 218 us
  blocking collectives  93.7 us (43%)
  Pallas kernels  79.1 us (36%)
  starting transfers between devices  18.7 us (9%)
  local copies, waits for them, and re-layouts  13.6 us (6%)
  waiting for transfers between devices  11.9 us (5%)
    all_to_all x1, blocking collectives, per_device(): lax.all_to_all(payload, ('stn', 'tm'), split_axis=0, concat_axis=0, tiled...  93.7 us
    pallas_call x3, Pallas kernels, filter_call(): pl.pallas_call(filter_body, name='filter', cost_estimate=pl.CostEstimate(...  40.1 us
    pallas_call x2, Pallas kernels, correlate_call(): pl.pallas_call(functools.partial(correlate_body, groups), name='correlate...  20.7 us
    pallas_call x1, Pallas kernels, spectrum_call(): pl.pallas_call(spectrum_body, name='spectrum', grid=(SLOTS // block,), in...  15.6 us
    ppermute x3, starting transfers between devices, per_device(): lax.ppermute(ends[0], 'tm', forward)  11.2 us
    slice x3, local copies, waits for them, and re-layouts, per_device(): ends = (block[:, frames - HALO:], block[:, :HALO])  9.75 us
    all_to_all x1, starting transfers between devices, per_device(): lax.all_to_all(payload, ('stn', 'tm'), split_axis=0, concat_axis=0, tiled...  6.35 us
    all_to_all x1, waiting for transfers between devices, per_device(): lax.all_to_all(payload, ('stn', 'tm'), split_axis=0, concat_axis=0, tiled...  6.32 us
  transfers between devices with their start and end apart: 7, of which 4 were waited for; matrix products, arithmetic and copies ran while one was open for 4% of the time, Pallas kernels for 22%

profile of v3, /device:TPU:1, one launch (start us, length us, event | category | flops | bytes accessed | tf_op | source)
XLA Modules:
  0.0 218.3 jit_solution(1157387728753310865)
XLA Ops:
  0.0 3.3 %fusion.2 = (bf16[24,8,4096]{2,1,0:T(8,128)(2,1)S(1)}, bf16[24,8,4096]{2,1,0:T(8,128)(2,1)}) fusion(bf16[64,16,4096]{2,1,0:T(8,128)(2,1)} %own_ref.5), kind=kLoop, calls=%fused_computation.5 | loop fusion | bytes 6291456 | tf_op jit(solution)/shard_map/slice | solution.py:409
  3.3 4.9 %collective-permute-start.4 = (bf16[24,8,4096]{2,1,0:T(8,128)(2,1)}, bf16[24,8,4096]{2,1,0:T(8,128)(2,1)}, u32[]{:S(2)}, u32[]{:S(2)}) collective-permute-start(bf16[24,8,4096]{2,1,0:T(8,128)(2,1)} %get-tuple-element.11), channel_id=1, source_target_pairs={{0,1},{1,2},{2,3},{3,4},{4,5},{5,6},{6,7},{7,8},{8,9},{9,10},{10,1... | collective-permute-start | bytes 4718600 | tf_op jit(solution)/shard_map/ppermute | solution.py:416
  8.2 0.1 collective-permute-start.5
  8.3 3.3 %fusion = (bf16[24,8,4096]{2,1,0:T(8,128)(2,1)S(1)}, bf16[24,8,4096]{2,1,0:T(8,128)(2,1)}) fusion(bf16[64,16,4096]{2,1,0:T(8,128)(2,1)} %own_ref.5), kind=kLoop, calls=%fused_computation.3 | loop fusion | bytes 6291456 | tf_op jit(solution)/shard_map/slice | solution.py:409
  11.6 3.6 %collective-permute-start.2 = (bf16[24,8,4096]{2,1,0:T(8,128)(2,1)}, bf16[24,8,4096]{2,1,0:T(8,128)(2,1)}, u32[]{:S(2)}, u32[]{:S(2)}) collective-permute-start(bf16[24,8,4096]{2,1,0:T(8,128)(2,1)} %get-tuple-element.16), channel_id=1, source_target_pairs={{0,1},{1,2},{2,3},{3,4},{4,5},{5,6},{6,7},{7,8},{8,9},{9,10},{10,1... | collective-permute-start | bytes 4718600 | tf_op jit(solution)/shard_map/ppermute | solution.py:416
  15.3 1.0 collective-permute-start.3
  16.3 3.1 %fusion.1 = (bf16[16,8,4096]{2,1,0:T(8,128)(2,1)}, bf16[16,8,4096]{2,1,0:T(8,128)(2,1)}) fusion(bf16[64,16,4096]{2,1,0:T(8,128)(2,1)} %own_ref.5), kind=kLoop, calls=%fused_computation.4 | loop fusion | bytes 4194304 | tf_op jit(solution)/shard_map/slice | solution.py:409
  19.4 2.7 %collective-permute-start = (bf16[16,8,4096]{2,1,0:T(8,128)(2,1)}, bf16[16,8,4096]{2,1,0:T(8,128)(2,1)}, u32[]{:S(2)}, u32[]{:S(2)}) collective-permute-start(bf16[16,8,4096]{2,1,0:T(8,128)(2,1)} %get-tuple-element.18), channel_id=1, source_target_pairs={{0,1},{1,2},{2,3},{3,4},{4,5},{5,6},{6,7},{7,8},{8,9},{9,10},{10,1... | collective-permute-start | bytes 3145736 | tf_op jit(solution)/shard_map/ppermute | solution.py:416
  22.1 2.8 %gains.1.gain_ref = f32[16,128,128]{2,1,0:T(8,128)} custom-call(f32[64,2048]{1,0:T(8,128)} %gain_ref.1), custom_call_target="tpu_custom_call" | custom-call | tf_op jit(solution)/shard_map/gains/pallas_call | solution.py:390
  24.9 1.0 collective-permute-done.4.before_ref
  25.9 0.0 collective-permute-start.1
  25.9 2.4 %collective-permute-done.5.after_ref = bf16[24,8,4096]{2,1,0:T(8,128)(2,1)} collective-permute-done((bf16[24,8,4096]{2,1,0:T(8,128)(2,1)S(1)}, bf16[24,8,4096]{2,1,0:T(8,128)(2,1)}, u32[]{:S(2)}, u32[]{:S(2)}) %collective-permute-start.5) | collective-permute-done | bytes 1572896 | tf_op jit(solution)/shard_map/ppermute | solution.py:416
  28.3 14.7 %filter.3.rest_0_ = f32[16,16,64,256]{3,2,1,0:T(8,128)} custom-call(f32[1]{0:T(128)} %bitcast.1.flag_ref, bf16[64,16,4096]{2,1,0:T(8,128)(2,1)} %own_ref.5, bf16[24,8,4096]{2,1,0:T(8,128)(2,1)} %collective-permute-done.4.before_ref, bf16[24,8,4096]{2,1,0:T(8,128)(2,1)} %collective-permute-done.5.after_ref, f32[16,4096]{1,0:T(8,128)} %taps_ref.5), custom_call_target="tpu_custom_call" | custom-call | flops 15000000512 | bytes 12582912 | tf_op jit(solution)/shard_map/filter/pallas_call | solution.py:141
  42.9 0.0 collective-permute-done.2.before_ref
  42.9 2.2 %collective-permute-done.3.after_ref = bf16[24,8,4096]{2,1,0:T(8,128)(2,1)} collective-permute-done((bf16[24,8,4096]{2,1,0:T(8,128)(2,1)S(1)}, bf16[24,8,4096]{2,1,0:T(8,128)(2,1)}, u32[]{:S(2)}, u32[]{:S(2)}) %collective-permute-start.3) | collective-permute-done | bytes 1572896 | tf_op jit(solution)/shard_map/ppermute | solution.py:416
  45.1 14.7 %filter.4.rest_0_ = f32[16,16,64,256]{3,2,1,0:T(8,128)} custom-call(f32[1]{0:T(128)} %bitcast.1.flag_ref, bf16[64,16,4096]{2,1,0:T(8,128)(2,1)} %own_ref.5, bf16[24,8,4096]{2,1,0:T(8,128)(2,1)} %collective-permute-done.2.before_ref, bf16[24,8,4096]{2,1,0:T(8,128)(2,1)} %collective-permute-done.3.after_ref, ...), custom_call_target="tpu_custom_call", output_to_operand_aliasing={{}: (5, {})} | custom-call | flops 15000000512 | bytes 12582912 | tf_op jit(solution)/shard_map/filter/pallas_call | solution.py:141
  59.8 0.0 collective-permute-done.before_ref
  59.8 0.0 collective-permute-done.1.after_ref
  59.8 1.0 copy-done.1
  60.8 10.8 %filter.5.part_ref = f32[16,16,64,256]{3,2,1,0:T(8,128)} custom-call(f32[1]{0:T(128)} %bitcast.1.flag_ref, bf16[64,16,4096]{2,1,0:T(8,128)(2,1)} %own_ref.5, bf16[16,8,4096]{2,1,0:T(8,128)(2,1)} %collective-permute-done.before_ref, bf16[16,8,4096]{2,1,0:T(8,128)(2,1)} %copy-done.1, f32[16,4096]{1,0:T(8,128)} %taps_ref.5, ...), custom_call_target="tpu_custom_call", output_to_operand_aliasing={{}: (5, {})} | custom-call | flops 10000000000 | bytes 8388608 | tf_op jit(solution)/shard_map/filter/pallas_call | solution.py:141
  71.5 15.6 %spectrum.1 = (bf16[128,27,8,128]{3,2,1,0:T(8,128)(2,1)}, bf16[128,6,8,128]{3,2,1,0:T(8,128)(2,1)}) custom-call(f32[16,16,64,256]{3,2,1,0:T(8,128)} %filter.5.part_ref, f32[128,128]{1,0:T(8,128)} %constant.39.clone.cos_ref, f32[128,128]{1,0:T(8,128)} %constant.40.clone.sin_ref, f32[16,2,128]{2,1,0:T(2,128)} %constant.41.clone.twist_cos_ref, ...), custom_call_target="tpu_custom_call" | custom-call | tf_op jit(solution)/shard_map/spectrum/pallas_call | solution.py:259
  87.1 93.7 %all_to_all.10.spec_ref = bf16[128,27,8,128]{3,2,1,0:T(8,128)(2,1)} all-to-all(bf16[128,27,8,128]{3,2,1,0:T(8,128)(2,1)} %get-tuple-element.14), channel_id=1, replica_groups=mesh['stn'=8,'tm'=16] {'stn','tm'}, dimensions={0} | all-to-all | bytes 14155776 | tf_op jit(solution)/shard_map/all_to_all | solution.py:426
  180.8 6.3 %all-to-all-start = ((bf16[128,6,8,128]{3,2,1,0:T(8,128)(2,1)}), bf16[128,6,8,128]{3,2,1,0:T(8,128)(2,1)S(1)}, u32[]{:S(2)}, u32[]{:S(2)}) async-start(bf16[128,6,8,128]{3,2,1,0:T(8,128)(2,1)} %get-tuple-element.13), calls=%async_computation | async-start | bytes 3145728 | tf_op jit(solution)/shard_map/all_to_all | solution.py:426
  187.2 1.1 convert_reduce_fusion
  188.3 0.1 reduce_sum.14
  188.4 0.1 reduce_sum.18
  188.5 0.9 rsqrt.23.col_ref
  189.4 0.7 div.18.row_ref
  190.1 15.7 %correlate.2.rest_0_ = f32[16,512,512]{2,1,0:T(8,128)} custom-call(s32[1]{0:T(128)} %bitcast.odd_ref, bf16[128,27,8,128]{3,2,1,0:T(8,128)(2,1)} %all_to_all.10.spec_ref, f32[1,512]{1,0:T(1,128)} %div.18.row_ref, f32[512,1]{1,0:T(8,128)} %rsqrt.23.col_ref), custom_call_target="tpu_custom_call" | custom-call | tf_op jit(solution)/shard_map/correlate/pallas_call | solution.py:344
  205.9 6.3 %all-to-all-done.spec_ref = bf16[128,6,8,128]{3,2,1,0:T(8,128)(2,1)S(1)} async-done(((bf16[128,6,8,128]{3,2,1,0:T(8,128)(2,1)}), bf16[128,6,8,128]{3,2,1,0:T(8,128)(2,1)S(1)}, u32[]{:S(2)}, u32[]{:S(2)}) %all-to-all-start) | async-done | bytes 1572896 | tf_op jit(solution)/shard_map/all_to_all | solution.py:426
  212.2 1.1 copy-done
  213.3 4.9 %correlate.3 = f32[16,512,512]{2,1,0:T(8,128)} custom-call(s32[1]{0:T(128)} %bitcast.odd_ref, bf16[128,6,8,128]{3,2,1,0:T(8,128)(2,1)} %copy-done, f32[1,512]{1,0:T(1,128)} %div.18.row_ref, f32[512,1]{1,0:T(8,128)} %rsqrt.23.col_ref, f32[16,512,512]{2,1,0:T(8,128)} %correlate.2.rest_0_), custom_call_target="tpu_custom_call", output_to_operand_aliasing={{}: (4, {})} | custom-call | tf_op jit(solution)/shard_map/correlate/pallas_call | solution.py:344
  (3 shorter events, 0.0 us)
Async XLA Ops:
  3.3 22.6 %collective-permute-start.4 = (bf16[24,8,4096]{2,1,0:T(8,128)(2,1)}, bf16[24,8,4096]{2,1,0:T(8,128)(2,1)}, u32[]{:S(2)}, u32[]{:S(2)}) collective-permute-start(bf16[24,8,4096]{2,1,0:T(8,128)(2,1)} %get-tuple-element.11), channel_id=1, source_target_pairs={{0,1},{1,2},{2,3},{3,4},{4,5},{5,6},{6,7},{7,8},{8,9},{9,10},{10,1... | collective-permute-start | bytes 4718600 | tf_op jit(solution)/shard_map/ppermute | solution.py:416
  8.2 20.0 %collective-permute-start.5 = (bf16[24,8,4096]{2,1,0:T(8,128)(2,1)S(1)}, bf16[24,8,4096]{2,1,0:T(8,128)(2,1)}, u32[]{:S(2)}, u32[]{:S(2)}) collective-permute-start(bf16[24,8,4096]{2,1,0:T(8,128)(2,1)S(1)} %get-tuple-element.12), channel_id=1, source_target_pairs={{1,0},{2,1},{3,2},{4,3},{5,4},{6,5},{7,6},{8,7},{9,8},{10,9},{11,1... | collective-permute-start | bytes 4718600 | tf_op jit(solution)/shard_map/ppermute | solution.py:416
  11.6 31.3 %collective-permute-start.2 = (bf16[24,8,4096]{2,1,0:T(8,128)(2,1)}, bf16[24,8,4096]{2,1,0:T(8,128)(2,1)}, u32[]{:S(2)}, u32[]{:S(2)}) collective-permute-start(bf16[24,8,4096]{2,1,0:T(8,128)(2,1)} %get-tuple-element.16), channel_id=1, source_target_pairs={{0,1},{1,2},{2,3},{3,4},{4,5},{5,6},{6,7},{7,8},{8,9},{9,10},{10,1... | collective-permute-start | bytes 4718600 | tf_op jit(solution)/shard_map/ppermute | solution.py:416
  15.3 29.8 %collective-permute-start.3 = (bf16[24,8,4096]{2,1,0:T(8,128)(2,1)S(1)}, bf16[24,8,4096]{2,1,0:T(8,128)(2,1)}, u32[]{:S(2)}, u32[]{:S(2)}) collective-permute-start(bf16[24,8,4096]{2,1,0:T(8,128)(2,1)S(1)} %get-tuple-element.15), channel_id=1, source_target_pairs={{1,0},{2,1},{3,2},{4,3},{5,4},{6,5},{7,6},{8,7},{9,8},{10,9},{11,1... | collective-permute-start | bytes 4718600 | tf_op jit(solution)/shard_map/ppermute | solution.py:416
  19.4 40.3 %collective-permute-start = (bf16[16,8,4096]{2,1,0:T(8,128)(2,1)}, bf16[16,8,4096]{2,1,0:T(8,128)(2,1)}, u32[]{:S(2)}, u32[]{:S(2)}) collective-permute-start(bf16[16,8,4096]{2,1,0:T(8,128)(2,1)} %get-tuple-element.18), channel_id=1, source_target_pairs={{0,1},{1,2},{2,3},{3,4},{4,5},{5,6},{6,7},{7,8},{8,9},{9,10},{10,1... | collective-permute-start | bytes 3145736 | tf_op jit(solution)/shard_map/ppermute | solution.py:416
  25.9 33.9 %collective-permute-start.1 = (bf16[16,8,4096]{2,1,0:T(8,128)(2,1)}, bf16[16,8,4096]{2,1,0:T(8,128)(2,1)S(1)}, u32[]{:S(2)}, u32[]{:S(2)}) collective-permute-start(bf16[16,8,4096]{2,1,0:T(8,128)(2,1)} %get-tuple-element.17), channel_id=1, source_target_pairs={{1,0},{2,1},{3,2},{4,3},{5,4},{6,5},{7,6},{8,7},{9,8},{10,9},{11,1... | collective-permute-start | bytes 3145736 | tf_op jit(solution)/shard_map/ppermute | solution.py:416
  59.8 1.0 copy-start.1
  180.8 31.4 %all-to-all-start = ((bf16[128,6,8,128]{3,2,1,0:T(8,128)(2,1)}), bf16[128,6,8,128]{3,2,1,0:T(8,128)(2,1)S(1)}, u32[]{:S(2)}, u32[]{:S(2)}) async-start(bf16[128,6,8,128]{3,2,1,0:T(8,128)(2,1)} %get-tuple-element.13), calls=%async_computation | async-start | bytes 3145728 | tf_op jit(solution)/shard_map/all_to_all | solution.py:426
  212.2 1.1 copy-start

commit v4 on v3

--- a/solution.py
+++ b/solution.py
@@ -153,7 +153,7 @@
             pltpu.VMEM((frames, tiles, GROUP, LANES), jnp.float32),
         ],
         input_output_aliases=aliases,
-        compiler_params=pltpu.CompilerParams(vmem_limit_bytes=56 * 2**20),
+        compiler_params=pltpu.CompilerParams(vmem_limit_bytes=49 * 2**20),
     )(*operands)
 
 
@@ -356,7 +356,7 @@
         ),
         out_shape=jax.ShapeDtypeStruct((channels, total, total), jnp.float32),
         input_output_aliases=aliases,
-        compiler_params=pltpu.CompilerParams(vmem_limit_bytes=56 * 2**20),
+        compiler_params=pltpu.CompilerParams(vmem_limit_bytes=20 * 2**20),
     )(*operands)
 
 

time: 219 us -> 215 us (0.982)
  Pallas kernels: 79.1 us -> 72.9 us
    pallas_call x2, Pallas kernels: 20.7 us -> 15.8 us  [correlate_call(): pl.pallas_call(functools.partial(correlate_body, groups), name='correlate...]
  transfers between devices with their start and end apart: 7 -> 7, of which waited for: 4 -> 5; matrix products, arithmetic and copies ran while one was open for 4% -> 4% of each run, Pallas kernels for 22% -> 20%
where the time goes in v4:
time: 215 us
  blocking collectives  93.7 us (44%)
  Pallas kernels  72.9 us (34%)
  starting transfers between devices  18.8 us (9%)
  local copies, waits for them, and re-layouts  14.3 us (7%)
  waiting for transfers between devices  13.6 us (6%)
    all_to_all x1, blocking collectives, per_device(): lax.all_to_all(payload, ('stn', 'tm'), split_axis=0, concat_axis=0, tiled...  93.7 us
    pallas_call x3, Pallas kernels, filter_call(): pl.pallas_call(filter_body, name='filter', cost_estimate=pl.CostEstimate(...  38.8 us
    pallas_call x2, Pallas kernels, correlate_call(): pl.pallas_call(functools.partial(correlate_body, groups), name='correlate...  15.8 us
    pallas_call x1, Pallas kernels, spectrum_call(): pl.pallas_call(spectrum_body, name='spectrum', grid=(SLOTS // block,), in...  15.6 us
    ppermute x3, starting transfers between devices, per_device(): lax.ppermute(ends[0], 'tm', forward)  11.3 us
    slice x3, local copies, waits for them, and re-layouts, per_device(): ends = (block[:, frames - HALO:], block[:, :HALO])  10.9 us
    all_to_all x1, waiting for transfers between devices, per_device(): lax.all_to_all(payload, ('stn', 'tm'), split_axis=0, concat_axis=0, tiled...  8 us
    all_to_all x1, starting transfers between devices, per_device(): lax.all_to_all(payload, ('stn', 'tm'), split_axis=0, concat_axis=0, tiled...  6.35 us
  transfers between devices with their start and end apart: 7, of which 5 were waited for; matrix products, arithmetic and copies ran while one was open for 4% of the time, Pallas kernels for 20%

profile of v4, /device:TPU:1, one launch (start us, length us, event | category | flops | bytes accessed | tf_op | source)
XLA Modules:
  0.0 214.6 jit_solution(12611911280688242836)
XLA Ops:
  0.0 3.9 %fusion.2 = (bf16[24,8,4096]{2,1,0:T(8,128)(2,1)}, bf16[24,8,4096]{2,1,0:T(8,128)(2,1)}) fusion(bf16[64,16,4096]{2,1,0:T(8,128)(2,1)} %own_ref.5), kind=kLoop, calls=%fused_computation.5 | loop fusion | bytes 6291456 | tf_op jit(solution)/shard_map/slice | solution.py:409
  3.9 4.9 %collective-permute-start.4 = (bf16[24,8,4096]{2,1,0:T(8,128)(2,1)}, bf16[24,8,4096]{2,1,0:T(8,128)(2,1)S(1)}, u32[]{:S(2)}, u32[]{:S(2)}) collective-permute-start(bf16[24,8,4096]{2,1,0:T(8,128)(2,1)} %get-tuple-element.11), channel_id=1, source_target_pairs={{0,1},{1,2},{2,3},{3,4},{4,5},{5,6},{6,7},{7,8},{8,9},{9,10},{10,1... | collective-permute-start | bytes 4718600 | tf_op jit(solution)/shard_map/ppermute | solution.py:416
  8.8 0.1 collective-permute-start.5
  8.9 3.9 %fusion = (bf16[24,8,4096]{2,1,0:T(8,128)(2,1)}, bf16[24,8,4096]{2,1,0:T(8,128)(2,1)}) fusion(bf16[64,16,4096]{2,1,0:T(8,128)(2,1)} %own_ref.5), kind=kLoop, calls=%fused_computation.3 | loop fusion | bytes 6291456 | tf_op jit(solution)/shard_map/slice | solution.py:409
  12.8 3.6 %collective-permute-start.2 = (bf16[24,8,4096]{2,1,0:T(8,128)(2,1)}, bf16[24,8,4096]{2,1,0:T(8,128)(2,1)}, u32[]{:S(2)}, u32[]{:S(2)}) collective-permute-start(bf16[24,8,4096]{2,1,0:T(8,128)(2,1)} %get-tuple-element.16), channel_id=1, source_target_pairs={{0,1},{1,2},{2,3},{3,4},{4,5},{5,6},{6,7},{7,8},{8,9},{9,10},{10,1... | collective-permute-start | bytes 4718600 | tf_op jit(solution)/shard_map/ppermute | solution.py:416
  16.4 1.1 collective-permute-start.3
  17.5 3.1 %fusion.1 = (bf16[16,8,4096]{2,1,0:T(8,128)(2,1)}, bf16[16,8,4096]{2,1,0:T(8,128)(2,1)}) fusion(bf16[64,16,4096]{2,1,0:T(8,128)(2,1)} %own_ref.5), kind=kLoop, calls=%fused_computation.4 | loop fusion | bytes 4194304 | tf_op jit(solution)/shard_map/slice | solution.py:409
  20.6 2.8 %collective-permute-start = (bf16[16,8,4096]{2,1,0:T(8,128)(2,1)}, bf16[16,8,4096]{2,1,0:T(8,128)(2,1)S(1)}, u32[]{:S(2)}, u32[]{:S(2)}) collective-permute-start(bf16[16,8,4096]{2,1,0:T(8,128)(2,1)} %get-tuple-element.18), channel_id=1, source_target_pairs={{0,1},{1,2},{2,3},{3,4},{4,5},{5,6},{6,7},{7,8},{8,9},{9,10},{10,1... | collective-permute-start | bytes 3145736 | tf_op jit(solution)/shard_map/ppermute | solution.py:416
  23.4 2.8 %gains.1.gain_ref = f32[16,128,128]{2,1,0:T(8,128)} custom-call(f32[64,2048]{1,0:T(8,128)} %gain_ref.1), custom_call_target="tpu_custom_call" | custom-call | tf_op jit(solution)/shard_map/gains/pallas_call | solution.py:390
  26.2 0.3 collective-permute-done.4.before_ref
  26.5 0.0 collective-permute-start.1
  26.5 2.6 %collective-permute-done.5.after_ref = bf16[24,8,4096]{2,1,0:T(8,128)(2,1)} collective-permute-done((bf16[24,8,4096]{2,1,0:T(8,128)(2,1)}, bf16[24,8,4096]{2,1,0:T(8,128)(2,1)}, u32[]{:S(2)}, u32[]{:S(2)}) %collective-permute-start.5) | collective-permute-done | bytes 1572896 | tf_op jit(solution)/shard_map/ppermute | solution.py:416
  29.1 0.0 copy-done.1
  29.1 14.2 %filter.3.rest_0_ = f32[16,16,64,256]{3,2,1,0:T(8,128)} custom-call(f32[1]{0:T(128)} %bitcast.1.flag_ref, bf16[64,16,4096]{2,1,0:T(8,128)(2,1)} %own_ref.5, bf16[24,8,4096]{2,1,0:T(8,128)(2,1)S(1)} %collective-permute-done.4.before_ref, bf16[24,8,4096]{2,1,0:T(8,128)(2,1)} %collective-permute-done.5.after_ref, f32[16,4096]{1,0:T(8,128)S(1)} %copy-done.1), custom_call_target="tpu_custom_call" | custom-call | flops 15000000512 | bytes 12582912 | tf_op jit(solution)/shard_map/filter/pallas_call | solution.py:141
  43.3 0.1 collective-permute-done.2.before_ref
  43.3 2.6 %collective-permute-done.3.after_ref = bf16[24,8,4096]{2,1,0:T(8,128)(2,1)} collective-permute-done((bf16[24,8,4096]{2,1,0:T(8,128)(2,1)}, bf16[24,8,4096]{2,1,0:T(8,128)(2,1)}, u32[]{:S(2)}, u32[]{:S(2)}) %collective-permute-start.3) | collective-permute-done | bytes 1572896 | tf_op jit(solution)/shard_map/ppermute | solution.py:416
  45.9 14.4 %filter.4.rest_0_ = f32[16,16,64,256]{3,2,1,0:T(8,128)} custom-call(f32[1]{0:T(128)} %bitcast.1.flag_ref, bf16[64,16,4096]{2,1,0:T(8,128)(2,1)} %own_ref.5, bf16[24,8,4096]{2,1,0:T(8,128)(2,1)} %collective-permute-done.2.before_ref, bf16[24,8,4096]{2,1,0:T(8,128)(2,1)} %collective-permute-done.3.after_ref, ...), custom_call_target="tpu_custom_call", output_to_operand_aliasing={{}: (5, {})} | custom-call | flops 15000000512 | bytes 12582912 | tf_op jit(solution)/shard_map/filter/pallas_call | solution.py:141
  60.3 0.0 collective-permute-done.before_ref
  60.3 0.0 collective-permute-done.1.after_ref
  60.3 10.2 %filter.5.part_ref = f32[16,16,64,256]{3,2,1,0:T(8,128)} custom-call(f32[1]{0:T(128)} %bitcast.1.flag_ref, bf16[64,16,4096]{2,1,0:T(8,128)(2,1)} %own_ref.5, bf16[16,8,4096]{2,1,0:T(8,128)(2,1)S(1)} %collective-permute-done.before_ref, bf16[16,8,4096]{2,1,0:T(8,128)(2,1)S(1)} %collective-permute-done.1.after_ref, ...), custom_call_target="tpu_custom_call", output_to_operand_aliasing={{}: (5, {})} | custom-call | flops 10000000000 | bytes 8388608 | tf_op jit(solution)/shard_map/filter/pallas_call | solution.py:141
  70.5 15.6 %spectrum.1 = (bf16[128,27,8,128]{3,2,1,0:T(8,128)(2,1)}, bf16[128,6,8,128]{3,2,1,0:T(8,128)(2,1)}) custom-call(f32[16,16,64,256]{3,2,1,0:T(8,128)} %filter.5.part_ref, f32[128,128]{1,0:T(8,128)} %constant.39.clone.cos_ref, f32[128,128]{1,0:T(8,128)} %constant.40.clone.sin_ref, f32[16,2,128]{2,1,0:T(2,128)} %constant.41.clone.twist_cos_ref, ...), custom_call_target="tpu_custom_call" | custom-call | tf_op jit(solution)/shard_map/spectrum/pallas_call | solution.py:259
  86.1 93.7 %all_to_all.10.spec_ref = bf16[128,27,8,128]{3,2,1,0:T(8,128)(2,1)} all-to-all(bf16[128,27,8,128]{3,2,1,0:T(8,128)(2,1)} %get-tuple-element.14), channel_id=1, replica_groups=mesh['stn'=8,'tm'=16] {'stn','tm'}, dimensions={0} | all-to-all | bytes 14155776 | tf_op jit(solution)/shard_map/all_to_all | solution.py:426
  179.8 6.3 %all-to-all-start = ((bf16[128,6,8,128]{3,2,1,0:T(8,128)(2,1)}), bf16[128,6,8,128]{3,2,1,0:T(8,128)(2,1)S(1)}, u32[]{:S(2)}, u32[]{:S(2)}) async-start(bf16[128,6,8,128]{3,2,1,0:T(8,128)(2,1)} %get-tuple-element.13), calls=%async_computation | async-start | bytes 3145728 | tf_op jit(solution)/shard_map/all_to_all | solution.py:426
  186.2 1.1 convert_reduce_fusion
  187.3 0.1 reduce_sum.14
  187.5 0.1 reduce_sum.18
  187.5 0.2 rsqrt.23.col_ref
  187.8 0.1 div.18.row_ref
  187.8 3.0 %copy-done = bf16[128,27,8,128]{3,2,1,0:T(8,128)(2,1)S(1)} copy-done((bf16[128,27,8,128]{3,2,1,0:T(8,128)(2,1)S(1)}, bf16[128,27,8,128]{3,2,1,0:T(8,128)(2,1)}, u32[]{:S(2)}) %copy-start) | copy-done | bytes 7077912
  190.8 12.4 %correlate.2.rest_0_ = f32[16,512,512]{2,1,0:T(8,128)} custom-call(s32[1]{0:T(128)} %bitcast.odd_ref, bf16[128,27,8,128]{3,2,1,0:T(8,128)(2,1)S(1)} %copy-done, f32[1,512]{1,0:T(1,128)S(1)} %div.18.row_ref, f32[512,1]{1,0:T(8,128)S(1)} %rsqrt.23.col_ref), custom_call_target="tpu_custom_call" | custom-call | tf_op jit(solution)/shard_map/correlate/pallas_call | solution.py:344
  203.2 8.0 %all-to-all-done.spec_ref = bf16[128,6,8,128]{3,2,1,0:T(8,128)(2,1)S(1)} async-done(((bf16[128,6,8,128]{3,2,1,0:T(8,128)(2,1)}), bf16[128,6,8,128]{3,2,1,0:T(8,128)(2,1)S(1)}, u32[]{:S(2)}, u32[]{:S(2)}) %all-to-all-start) | async-done | bytes 1572896 | tf_op jit(solution)/shard_map/all_to_all | solution.py:426
  211.2 3.4 %correlate.3 = f32[16,512,512]{2,1,0:T(8,128)} custom-call(s32[1]{0:T(128)} %bitcast.odd_ref, bf16[128,6,8,128]{3,2,1,0:T(8,128)(2,1)S(1)} %all-to-all-done.spec_ref, f32[1,512]{1,0:T(1,128)S(1)} %div.18.row_ref, f32[512,1]{1,0:T(8,128)S(1)} %rsqrt.23.col_ref, f32[16,512,512]{2,1,0:T(8,128)} %correlate.2.rest_0_), custom_call_target="tpu_custom_call", output_to_operand_aliasing={{}: (4, {})} | custom-call | tf_op jit(solution)/shard_map/correlate/pallas_call | solution.py:344
  (3 shorter events, 0.0 us)
Async XLA Ops:
  3.9 22.6 %collective-permute-start.4 = (bf16[24,8,4096]{2,1,0:T(8,128)(2,1)}, bf16[24,8,4096]{2,1,0:T(8,128)(2,1)S(1)}, u32[]{:S(2)}, u32[]{:S(2)}) collective-permute-start(bf16[24,8,4096]{2,1,0:T(8,128)(2,1)} %get-tuple-element.11), channel_id=1, source_target_pairs={{0,1},{1,2},{2,3},{3,4},{4,5},{5,6},{6,7},{7,8},{8,9},{9,10},{10,1... | collective-permute-start | bytes 4718600 | tf_op jit(solution)/shard_map/ppermute | solution.py:416
  8.8 20.2 %collective-permute-start.5 = (bf16[24,8,4096]{2,1,0:T(8,128)(2,1)}, bf16[24,8,4096]{2,1,0:T(8,128)(2,1)}, u32[]{:S(2)}, u32[]{:S(2)}) collective-permute-start(bf16[24,8,4096]{2,1,0:T(8,128)(2,1)} %get-tuple-element.12), channel_id=1, source_target_pairs={{1,0},{2,1},{3,2},{4,3},{5,4},{6,5},{7,6},{8,7},{9,8},{10,9},{11,1... | collective-permute-start | bytes 4718600 | tf_op jit(solution)/shard_map/ppermute | solution.py:416
  12.8 30.5 %collective-permute-start.2 = (bf16[24,8,4096]{2,1,0:T(8,128)(2,1)}, bf16[24,8,4096]{2,1,0:T(8,128)(2,1)}, u32[]{:S(2)}, u32[]{:S(2)}) collective-permute-start(bf16[24,8,4096]{2,1,0:T(8,128)(2,1)} %get-tuple-element.16), channel_id=1, source_target_pairs={{0,1},{1,2},{2,3},{3,4},{4,5},{5,6},{6,7},{7,8},{8,9},{9,10},{10,1... | collective-permute-start | bytes 4718600 | tf_op jit(solution)/shard_map/ppermute | solution.py:416
  16.4 29.5 %collective-permute-start.3 = (bf16[24,8,4096]{2,1,0:T(8,128)(2,1)}, bf16[24,8,4096]{2,1,0:T(8,128)(2,1)}, u32[]{:S(2)}, u32[]{:S(2)}) collective-permute-start(bf16[24,8,4096]{2,1,0:T(8,128)(2,1)} %get-tuple-element.15), channel_id=1, source_target_pairs={{1,0},{2,1},{3,2},{4,3},{5,4},{6,5},{7,6},{8,7},{9,8},{10,9},{11,1... | collective-permute-start | bytes 4718600 | tf_op jit(solution)/shard_map/ppermute | solution.py:416
  20.6 8.5 %copy-start.1 = (f32[16,4096]{1,0:T(8,128)S(1)}, f32[16,4096]{1,0:T(8,128)}, u32[]{:S(2)}) copy-start(f32[16,4096]{1,0:T(8,128)} %taps_ref.5) | copy-start | bytes 786436
  20.6 39.7 %collective-permute-start = (bf16[16,8,4096]{2,1,0:T(8,128)(2,1)}, bf16[16,8,4096]{2,1,0:T(8,128)(2,1)S(1)}, u32[]{:S(2)}, u32[]{:S(2)}) collective-permute-start(bf16[16,8,4096]{2,1,0:T(8,128)(2,1)} %get-tuple-element.18), channel_id=1, source_target_pairs={{0,1},{1,2},{2,3},{3,4},{4,5},{5,6},{6,7},{7,8},{8,9},{9,10},{10,1... | collective-permute-start | bytes 3145736 | tf_op jit(solution)/shard_map/ppermute | solution.py:416
  26.5 33.8 %collective-permute-start.1 = (bf16[16,8,4096]{2,1,0:T(8,128)(2,1)}, bf16[16,8,4096]{2,1,0:T(8,128)(2,1)S(1)}, u32[]{:S(2)}, u32[]{:S(2)}) collective-permute-start(bf16[16,8,4096]{2,1,0:T(8,128)(2,1)} %get-tuple-element.17), channel_id=1, source_target_pairs={{1,0},{2,1},{3,2},{4,3},{5,4},{6,5},{7,6},{8,7},{9,8},{10,9},{11,1... | collective-permute-start | bytes 3145736 | tf_op jit(solution)/shard_map/ppermute | solution.py:416
  179.8 31.4 %all-to-all-start = ((bf16[128,6,8,128]{3,2,1,0:T(8,128)(2,1)}), bf16[128,6,8,128]{3,2,1,0:T(8,128)(2,1)S(1)}, u32[]{:S(2)}, u32[]{:S(2)}) async-start(bf16[128,6,8,128]{3,2,1,0:T(8,128)(2,1)} %get-tuple-element.13), calls=%async_computation | async-start | bytes 3145728 | tf_op jit(solution)/shard_map/all_to_all | solution.py:426
  187.8 3.0 %copy-start = (bf16[128,27,8,128]{3,2,1,0:T(8,128)(2,1)S(1)}, bf16[128,27,8,128]{3,2,1,0:T(8,128)(2,1)}, u32[]{:S(2)}) copy-start(bf16[128,27,8,128]{3,2,1,0:T(8,128)(2,1)} %all_to_all.10.spec_ref) | copy-start | bytes 21233668
